TPU v7x, 32 devices: a whole 2x2x4 slice. The times are simulated.
32 devices in a mesh: dp: 16 (over z, y, x), expert: 2 (over core).
Axes of the slice: x: 2, y: 2, z: 4, core: 2. Of those that a mesh axis runs over, the one named last changes fastest.
Arguments:
- latents: bfloat16 [4096, 2048], P('dp', 'expert'), as said below
- cotangent: bfloat16 [4096, 2048], P('dp', 'expert'), may hold values from -6 to 6
- routes: int32 [4096, 2], P('dp'), may hold values from 0 to 15, all different within a row; in each aligned block of 256 rows (0 to 255, 256 to 511, ...) at most 48 rows name the same one
- router_w: float32 [2048, 16], P('expert'), may hold values from -1 to 1
- mod_shift: bfloat16 [1, 2048], P(None, 'expert'), may hold values from -3 to 3
- mod_scale: bfloat16 [1, 2048], P(None, 'expert'), may hold values from -1.5 to 2.5
- mod_gate: bfloat16 [1, 2048], P(None, 'expert'), may hold values from -4 to 4
- gate_w: bfloat16 [16, 2048, 1024], P('dp', None, 'expert'), may hold values from -0.125 to 0.125
- up_w: bfloat16 [16, 2048, 1024], P('dp', None, 'expert'), may hold values from -0.125 to 0.125
- down_w: bfloat16 [16, 1024, 2048], P('dp', 'expert'), may hold values from -0.1875 to 0.1875
Outputs:
- latent_gradient: bfloat16 [4096, 2048], P('dp', 'expert')
- grad_gate_w: bfloat16 [16, 2048, 1024], P('dp', None, 'expert')
- grad_up_w: bfloat16 [16, 2048, 1024], P('dp', None, 'expert')
- grad_down_w: bfloat16 [16, 1024, 2048], P('dp', 'expert')
- grad_router: float32 [2048, 16], P('expert')
Inputs may be any that keep to these rules, and one draw needn't show every extreme that they name: `routes`: the two experts of a token differ. Among the 256 tokens of one aligned block (the tokens of one index of dp), no expert is named more than 48 times, a bound that some block reaches. Columns and rows of latents have unlike scales.
All inputs are finite; a program needn't handle non-finite values.
Results may differ from a plain program's by a relative error of at most 0.008.
Values may be sent and summed in bfloat16 or wider, within the bound.
No kernel may reach another device: no remote copies, remote signals or barrier semaphores. Data moves between devices by JAX's collectives and lax.ppermute only.
A program may use at most 128 MiB of HBM per device.

v0:
```python
import jax
import jax.numpy as jnp
from jax import lax
from jax.sharding import PartitionSpec as P

SEQ = 4096


norm_eps = 1e-06


def slot_targets(routes, experts, capacity):
    flat_routes = routes.reshape(-1)
    expert_ids = jnp.arange(experts, dtype=jnp.int32)
    onehot = (flat_routes[:, None] == expert_ids[None, :]).astype(jnp.int32)
    rank_run = jnp.cumsum(onehot, axis=0) - 1
    return flat_routes * capacity + jnp.sum(onehot * rank_run, axis=1)


def selected_row(table, sample_index):
    return lax.dynamic_slice_in_dim(table, sample_index, 1, 0).astype(jnp.float32)


def owner_view(arrived, groups, local):
    shaped = arrived.reshape((groups, local) + arrived.shape[1:])
    shaped = jnp.swapaxes(shaped, 0, 1)
    return shaped.reshape((local, groups * arrived.shape[1]) + arrived.shape[2:])


def sender_view(outgoing, groups):
    local = outgoing.shape[0]
    capacity = outgoing.shape[1] // groups
    shaped = outgoing.reshape((local, groups, capacity) + outgoing.shape[2:])
    shaped = jnp.swapaxes(shaped, 0, 1)
    return shaped.reshape((groups * local, capacity) + outgoing.shape[2:])


def route_weights(logits, routes, experts):
    chances = jax.nn.sigmoid(logits)
    expert_ids = jnp.arange(experts, dtype=jnp.int32)
    hits = routes[:, :, None] == expert_ids[None, None, :]
    picked = jnp.sum(jnp.where(hits, chances[:, None, :], 0.0), axis=2)
    pick_sum = jnp.sum(picked, axis=1, keepdims=True)
    return (hits, picked, pick_sum, picked / pick_sum)


def fill_slots(rows_b, scaled_dy, weights_b, targets, slot_count):
    width_here = rows_b.shape[1]
    send_x = (
        jnp.zeros((slot_count, width_here), jnp.bfloat16)
        .at[targets]
        .set(jnp.repeat(rows_b, 2, axis=0))
    )
    send_z = (
        jnp.zeros((slot_count, width_here), jnp.bfloat16)
        .at[targets]
        .set(jnp.repeat(scaled_dy, 2, axis=0))
    )
    send_w = jnp.zeros((slot_count,), jnp.bfloat16).at[targets].set(weights_b.reshape(-1))
    return (send_x, send_z, send_w)


def expert_grads(gate_lin, up_lin, down_back, slot_w):
    gate_sig = jax.nn.sigmoid(gate_lin)
    gate_act = gate_lin * gate_sig
    hidden = gate_act * up_lin
    slot_score = jnp.sum(hidden * down_back, axis=-1)
    d_gate = down_back * up_lin * gate_sig * (1.0 + gate_lin * (1.0 - gate_sig))
    d_up = down_back * gate_act
    scale_col = slot_w.astype(jnp.float32)[..., None]
    return (
        d_gate.astype(jnp.bfloat16),
        d_up.astype(jnp.bfloat16),
        slot_score,
        (scale_col * d_gate).astype(jnp.bfloat16),
        (scale_col * d_up).astype(jnp.bfloat16),
        (scale_col * hidden).astype(jnp.bfloat16),
    )


def weight_grads(rows_x, rows_z, gate_wt, up_wt, hidden_wt):
    grad_gate = jnp.einsum(
        "esd,esh->edh", rows_x, gate_wt, preferred_element_type=jnp.float32
    ).astype(jnp.bfloat16)
    grad_up = jnp.einsum("esd,esh->edh", rows_x, up_wt, preferred_element_type=jnp.float32).astype(
        jnp.bfloat16
    )
    grad_down = jnp.einsum(
        "esh,esd->ehd", hidden_wt, rows_z, preferred_element_type=jnp.float32
    ).astype(jnp.bfloat16)
    return (grad_gate, grad_up, grad_down)


def slot_total(slot_score):
    return lax.psum(slot_score, "expert")


def finish_tokens(
    returned_rows,
    score_rows,
    hits,
    picked,
    pick_sum,
    weights,
    normed_part,
    centered_scaled_slice,
    amp_part,
    inverse_deviation,
    output_gradient_slice,
    router_w,
    entire_width,
):
    highest = lax.Precision.HIGHEST
    tok_rows = weights.shape[0]
    paired = returned_rows.reshape(tok_rows, 2, -1)
    combined = weights[:, 0:1] * paired[:, 0] + weights[:, 1:2] * paired[:, 1]
    score_pair = score_rows.reshape(tok_rows, 2)
    mean_score = jnp.sum(weights * score_pair, axis=1, keepdims=True)
    d_pick = (score_pair - mean_score) / pick_sum * picked * (1.0 - picked)
    dlogit = jnp.sum(jnp.where(hits, d_pick[:, :, None], 0.0), axis=1)
    dnormed = combined + jnp.einsum("te,de->td", dlogit, router_w, precision=highest)
    grad_router = lax.psum(jnp.einsum("td,te->de", normed_part, dlogit, precision=highest), "dp")
    normalized_gradient = dnormed * amp_part
    first_sum, second_sum = lax.psum(
        (
            jnp.sum(normalized_gradient, axis=1, keepdims=True),
            jnp.sum(normalized_gradient * centered_scaled_slice, axis=1, keepdims=True),
        ),
        "expert",
    )
    latent_gradient = (
        inverse_deviation
        * (
            normalized_gradient
            - first_sum / entire_width
            - centered_scaled_slice * (second_sum / entire_width)
        )
        + output_gradient_slice
    )
    return (latent_gradient.astype(jnp.bfloat16), grad_router)


def per_device(
    latents, cotangent, routes, router_w, mod_shift, mod_scale, mod_gate, gate_w, up_w, down_w
):
    highest = lax.Precision.HIGHEST
    tok_rows = latents.shape[0]
    slice_width = latents.shape[1]
    experts = router_w.shape[1]
    local = gate_w.shape[0]
    groups = lax.axis_size("dp")
    entire_width = slice_width * lax.axis_size("expert")
    capacity = 3 * tok_rows // experts
    slot_count = experts * capacity
    sample_index = lax.axis_index("dp") * tok_rows // SEQ
    column_offset = lax.axis_index("expert") * slice_width
    targets = slot_targets(routes, experts, capacity)
    output_gradient_slice = cotangent.astype(jnp.float32)
    whole_x, whole_dy, entire_shift, whole_scale, whole_gate = (
        lax.all_gather(latents, "expert", axis=1, tiled=True),
        lax.all_gather(cotangent, "expert", axis=1, tiled=True),
        lax.all_gather(mod_shift, "expert", axis=1, tiled=True),
        lax.all_gather(mod_scale, "expert", axis=1, tiled=True),
        lax.all_gather(mod_gate, "expert", axis=1, tiled=True),
    )
    router_full = lax.all_gather(
        router_w.astype(jnp.bfloat16), "expert", axis=0, tiled=True
    ).astype(router_w.dtype)
    latent_rows_f32 = whole_x.astype(jnp.float32)
    row_average = jnp.mean(latent_rows_f32, axis=1, keepdims=True)
    row_msq = jnp.mean(latent_rows_f32 * latent_rows_f32, axis=1, keepdims=True)
    inverse_deviation = lax.rsqrt(row_msq - row_average * row_average + norm_eps)
    centered_scaled = (latent_rows_f32 - row_average) * inverse_deviation
    modulation_amplitude = 1.0 + selected_row(whole_scale, sample_index)
    normed_rows = centered_scaled * modulation_amplitude + selected_row(entire_shift, sample_index)
    normed_b = normed_rows.astype(jnp.bfloat16)
    logits = jnp.dot(normed_rows, router_full, precision=highest)
    hits, picked, pick_sum, weights = route_weights(logits, routes, experts)
    scaled_dy = (selected_row(whole_gate, sample_index) * whole_dy.astype(jnp.float32)).astype(
        jnp.bfloat16
    )
    send_x, send_z, send_w = fill_slots(
        normed_b, scaled_dy, weights.astype(jnp.bfloat16), targets, slot_count
    )
    got_x, got_z, got_w = (
        lax.all_to_all(
            send_x.reshape(experts, capacity, entire_width),
            "dp",
            split_axis=0,
            concat_axis=0,
            tiled=True,
        ),
        lax.all_to_all(
            send_z.reshape(experts, capacity, entire_width),
            "dp",
            split_axis=0,
            concat_axis=0,
            tiled=True,
        ),
        lax.all_to_all(
            send_w.reshape(experts, capacity), "dp", split_axis=0, concat_axis=0, tiled=True
        ),
    )
    rows_x = owner_view(got_x, groups, local)
    rows_z = owner_view(got_z, groups, local)
    slot_w = owner_view(got_w, groups, local)
    gate_lin = jnp.einsum("esd,edh->esh", rows_x, gate_w, preferred_element_type=jnp.float32)
    up_lin = jnp.einsum("esd,edh->esh", rows_x, up_w, preferred_element_type=jnp.float32)
    down_back = jnp.einsum("esd,ehd->esh", rows_z, down_w, preferred_element_type=jnp.float32)
    d_gate_b, d_up_b, slot_score, gate_wt, up_wt, hidden_wt = expert_grads(
        gate_lin, up_lin, down_back, slot_w
    )
    grad_gate, grad_up, grad_down = weight_grads(rows_x, rows_z, gate_wt, up_wt, hidden_wt)
    part_rows = (
        jnp.einsum("esh,edh->esd", d_gate_b, gate_w, preferred_element_type=jnp.float32)
        + jnp.einsum("esh,edh->esd", d_up_b, up_w, preferred_element_type=jnp.float32)
    ).astype(jnp.bfloat16)
    score_sum = slot_total(slot_score)
    back_rows = lax.all_to_all(
        sender_view(part_rows, groups), "dp", split_axis=0, concat_axis=0, tiled=True
    )
    back_scores = lax.all_to_all(
        sender_view(score_sum, groups), "dp", split_axis=0, concat_axis=0, tiled=True
    )
    summed = lax.psum_scatter(
        back_rows.reshape(slot_count, entire_width).astype(jnp.float32).astype(jnp.bfloat16),
        "expert",
        scatter_dimension=1,
        tiled=True,
    ).astype(jnp.float32)
    returned_rows = summed[targets]
    score_rows = back_scores.reshape(-1)[targets]
    centered_scaled_slice = lax.dynamic_slice_in_dim(centered_scaled, column_offset, slice_width, 1)
    amp_part = lax.dynamic_slice_in_dim(modulation_amplitude, column_offset, slice_width, 1)
    normed_part = lax.dynamic_slice_in_dim(normed_rows, column_offset, slice_width, 1)
    latent_gradient, grad_router = finish_tokens(
        returned_rows,
        score_rows,
        hits,
        picked,
        pick_sum,
        weights,
        normed_part,
        centered_scaled_slice,
        amp_part,
        inverse_deviation,
        output_gradient_slice,
        router_w,
        entire_width,
    )
    return (latent_gradient, grad_gate, grad_up, grad_down, grad_router)


def solution(mesh):
    placed = (
        P("dp", "expert"),
        P("dp", "expert"),
        P("dp", None),
        P("expert", None),
        P(None, "expert"),
        P(None, "expert"),
        P(None, "expert"),
        P("dp", None, "expert"),
        P("dp", None, "expert"),
        P("dp", "expert", None),
    )
    return jax.shard_map(
        per_device,
        mesh=mesh,
        in_specs=placed,
        out_specs=(
            P("dp", "expert"),
            P("dp", None, "expert"),
            P("dp", None, "expert"),
            P("dp", "expert", None),
            P("expert", None),
        ),
        check_vma=False,
    )
```

profile of v0, /device:TPU:0, one launch (start us, length us, event | category | flops | bytes accessed | tf_op | source)
XLA Modules:
  0.0 442.7 jit_solution(14642404818928266631)
XLA Ops:
  7.2 0.7 all-gather.3.cloned.1.call-update
  7.9 0.7 broadcast_multiply_fusion
  8.6 0.8 copy.35
  9.4 0.1 eq.45
  9.6 0.1 eq.41
  9.7 2.1 all_gather.20
  11.8 0.1 copy.34
  12.0 0.1 mul.200
  12.1 1.2 reduce-window.6
  13.3 0.2 slice_reduce_fusion
  13.5 1.9 all_gather.19
  15.6 5.7 %all-gather.3.cloned.1.call-done = bf16[256,2048]{1,0:T(8,128)(2,1)} async-done(((bf16[256,1024]{1,0:T(8,128)(2,1)}), bf16[256,2048]{1,0:T(8,128)(2,1)}) %all-gather.3.cloned.1.call-update) | async-done | bytes 1048592 | tf_op jit(solution)/shard_map/all_gather | solution.py:160
  21.3 1.7 convert_reduce_fusion
  23.0 3.8 multiply_add_fusion
  26.9 2.6 broadcast_in_dim.35
  29.4 4.1 reshape.288
  33.5 6.7 %scatter_custom_fusion.1 = bf16[768,2048]{1,0:T(8,128)(2,1)} fusion(s32[512]{0:T(512)S(1)} %bitcast.91, bf16[512,2048]{1,0:T(8,128)(2,1)} %reshape.288, bf16[]{:T(256)} %constant.21.clone.1), kind=kCustom, calls=%fused_computation.35 | custom fusion | bytes 3146240 | tf_op jit(solution)/shard_map/scatter | solution.py:52
  40.3 7.0 %all-to-all-start.1 = ((bf16[16,48,2048]{2,1,0:T(8,128)(2,1)}), bf16[16,48,2048]{2,1,0:T(8,128)(2,1)}, u32[]{:S(2)}, u32[]{:S(2)}) async-start(bf16[16,48,2048]{2,1,0:T(8,128)(2,1)} %bitcast.82), calls=%async_computation.1 | async-start | bytes 6291456 | tf_op jit(solution)/shard_map/all_to_all | solution.py:186
  47.3 0.7 all-gather.5.cloned.1.call-update
  48.0 2.3 all_gather.22
  50.4 9.5 %all-gather.5.cloned.1.call-done = bf16[256,2048]{1,0:T(8,128)(2,1)} async-done(((bf16[256,1024]{1,0:T(8,128)(2,1)}), bf16[256,2048]{1,0:T(8,128)(2,1)}) %all-gather.5.cloned.1.call-update) | async-done | bytes 1048592 | tf_op jit(solution)/shard_map/all_gather | solution.py:161
  59.9 1.5 multiply_convert_fusion
  61.4 2.6 broadcast_in_dim.34
  64.0 4.1 reshape.280
  68.1 6.7 %scatter_custom_fusion = bf16[768,2048]{1,0:T(8,128)(2,1)} fusion(s32[512]{0:T(512)S(1)} %bitcast.92, bf16[512,2048]{1,0:T(8,128)(2,1)} %reshape.280, bf16[]{:T(256)} %constant.21.clone.1), kind=kCustom, calls=%fused_computation.37 | custom fusion | bytes 3146240 | tf_op jit(solution)/shard_map/scatter | solution.py:57
  74.9 33.7 %all-to-all-done.1 = bf16[16,48,2048]{2,1,0:T(8,128)(2,1)} async-done(((bf16[16,48,2048]{2,1,0:T(8,128)(2,1)}), bf16[16,48,2048]{2,1,0:T(8,128)(2,1)}, u32[]{:S(2)}, u32[]{:S(2)}) %all-to-all-start.1) | async-done | bytes 3145760 | tf_op jit(solution)/shard_map/all_to_all | solution.py:186
  108.6 16.2 %all-to-all-start = ((bf16[16,48,2048]{2,1,0:T(8,128)(2,1)}), bf16[16,48,2048]{2,1,0:T(8,128)(2,1)}, u32[]{:S(2)}, u32[]{:S(2)}) async-start(bf16[16,48,2048]{2,1,0:T(8,128)(2,1)} %bitcast.83), calls=%async_computation | async-start | bytes 6291456 | tf_op jit(solution)/shard_map/all_to_all | solution.py:193
  124.8 0.2 reduce-scatter.2.cloned.1.call-start
  125.1 5.0 %fusion.7 = f32[768,512]{0,1:T(8,128)} fusion(bf16[768,2048]{1,0:T(8,128)(2,1)} %bitcast.11, bf16[1,2048,512]{2,1,0:T(8,128)(2,1)S(1)} %copy-done), kind=kOutput, calls=%fused_computation.19 | convolution fusion | flops 1610612736 | bytes 6815744 | tf_op jit(solution)/shard_map/esd,edh->esh/dot_general | solution.py:207
  130.1 4.9 %fusion.10 = f32[768,512]{0,1:T(8,128)} fusion(bf16[768,2048]{1,0:T(8,128)(2,1)} %bitcast.11, bf16[1,2048,512]{2,1,0:T(8,128)(2,1)S(1)} %copy-done.8), kind=kOutput, calls=%fused_computation.22 | convolution fusion | flops 1610612736 | bytes 6815744 | tf_op jit(solution)/shard_map/esd,edh->esh/dot_general | solution.py:208
  135.0 50.6 %all-to-all-done = bf16[16,48,2048]{2,1,0:T(8,128)(2,1)} async-done(((bf16[16,48,2048]{2,1,0:T(8,128)(2,1)}), bf16[16,48,2048]{2,1,0:T(8,128)(2,1)}, u32[]{:S(2)}, u32[]{:S(2)}) %all-to-all-start) | async-done | bytes 3145760 | tf_op jit(solution)/shard_map/all_to_all | solution.py:193
  185.5 5.5 %multiply_reduce_fusion = (f32[768]{0:T(1024)S(1)}, f32[768,512]{0,1:T(8,128)S(1)}) fusion(f32[768,512]{0,1:T(8,128)} %fusion.10, f32[768,512]{0,1:T(8,128)} %fusion.7, bf16[768,2048]{1,0:T(8,128)(2,1)} %bitcast.8, bf16[1,512,2048]{2,1,0:T(8,128)(2,1)} %param.19), kind=kOutput, calls=%fused_computation.31 | convolution fusion | flops 1613364480 | bytes 9964544 | tf_op jit(solution)/shard_map/esd,ehd->esh/dot_general | solution.py:209
  191.1 2.3 fusion.5
  193.4 1.9 add_convert_fusion
  195.4 84.8 %all_to_all.34 = bf16[16,48,2048]{2,1,0:T(8,128)(2,1)} all-to-all(bf16[16,48,2048]{2,1,0:T(8,128)(2,1)S(1)} %bitcast.84), channel_id=1, replica_groups=mesh['dp'=16,'expert'=2] {'dp'}, dimensions={0} | all-to-all | bytes 6291456 | tf_op jit(solution)/shard_map/all_to_all | solution.py:219
  280.2 0.8 copy-done.5
  281.0 2.1 all_gather.21
  283.1 1.5 fusion.22
  284.6 0.1 copy.42
  284.7 0.1 reshape.296
  284.9 3.8 scatter_custom_fusion.2
  288.7 0.7 all_to_all.28
  289.4 4.0 all-to-all-start.4
  293.4 7.2 %all-to-all-done.4 = bf16[16,1,48]{2,1,0:T(2,128)(2,1)S(1)} async-done(((bf16[16,1,48]{2,1,0:T(2,128)(2,1)}), bf16[16,1,48]{2,1,0:T(2,128)(2,1)S(1)}, u32[]{:S(2)}, u32[]{:S(2)}) %all-to-all-start.4) | async-done | bytes 1568 | tf_op jit(solution)/shard_map/all_to_all | solution.py:200
  300.8 3.1 psum.28
  303.9 3.5 all-to-all-start.3
  307.4 0.3 all-reduce.3.cloned.1.call-start
  307.7 6.3 %fusion.1 = bf16[1,2048,512]{2,1,0:T(8,128)(2,1)} fusion(bf16[768,2048]{1,0:T(8,128)(2,1)} %bitcast.11, f32[768]{0:T(1024)S(1)} %reshape.259, f32[768,512]{0,1:T(8,128)} %copy-done.12, f32[768,512]{0,1:T(8,128)} %fusion.7), kind=kOutput, calls=%fused_computation.13 | convolution fusion | flops 1614413824 | bytes 8391680 | tf_op jit(solution)/shard_map/esd,esh->edh/dot_general | solution.py:85
  314.0 5.2 %fusion = bf16[1,2048,512]{2,1,0:T(8,128)(2,1)} fusion(bf16[768,2048]{1,0:T(8,128)(2,1)} %bitcast.11, f32[768]{0:T(1024)S(1)} %reshape.259, f32[768,512]{0,1:T(8,128)S(1)} %copy-done.11, f32[768,512]{0,1:T(8,128)S(1)} %copy-done.13, f32[768,512]{0,1:T(8,128)S(1)} %copy-done.15), kind=kOutput, calls=%fused_computation.12 | convolution fusion | flops 1615986688 | bytes 9964544 | tf_op jit(solution)/shard_map/esd,esh->edh/dot_general | solution.py:82
  319.2 5.1 %fusion.2 = bf16[1,512,2048]{2,1,0:T(8,128)(2,1)} fusion(bf16[768,2048]{1,0:T(8,128)(2,1)} %bitcast.8, f32[768]{0:T(1024)S(1)} %reshape.259, f32[768,512]{0,1:T(8,128)S(1)} %copy-done.15, f32[768,512]{0,1:T(8,128)S(1)} %copy-done.11), kind=kOutput, calls=%fused_computation.14 | convolution fusion | flops 1614413824 | bytes 8391680 | tf_op jit(solution)/shard_map/esh,esd->ehd/dot_general | solution.py:88
  324.3 0.5 broadcast.185
  324.8 0.8 reduce.12
  325.7 2.3 gather_fusion.1
  327.9 0.1 reshape.255
  328.2 1.3 fusion.26
  329.6 1.8 convert_element_type.108
  331.4 2.7 gather_fusion
  334.1 2.5 reshape.253
  336.6 1.6 fusion.49
  338.3 1.5 fusion.47
  339.8 2.5 all-reduce
  342.3 2.5 add_convert_fusion.1
  344.8 89.7 %all-reduce.3.cloned.1.call-done = f32[1024,16]{0,1:T(8,128)} async-done(((f32[1024,16]{0,1:T(8,128)}), f32[1024,16]{0,1:T(8,128)}) %all-reduce.3.cloned.1.call-update) | async-done | bytes 65552 | tf_op jit(solution)/shard_map/psum | solution.py:122
  434.4 1.5 copy.61
  (61 shorter events, 0.8 us)
Async XLA Ops:
  7.2 117.9 %copy-start = (bf16[1,2048,512]{2,1,0:T(8,128)(2,1)S(1)}, bf16[1,2048,512]{2,1,0:T(8,128)(2,1)}, u32[]{:S(2)}) copy-start(bf16[1,2048,512]{2,1,0:T(8,128)(2,1)} %param.17) | copy-start | bytes 6291460
  7.2 14.1 %all-gather.3.cloned.1.call-start = ((), (), s32[]{:S(2)}) async-start(), calls=%async_computation.6 | async-start | bytes 1572864 | tf_op jit(solution)/shard_map/all_gather | solution.py:160
  40.3 7.7 %copy-start.7 = (bf16[1,1024]{1,0:T(2,128)(2,1)S(1)}, bf16[1,1024]{1,0:T(2,128)(2,1)}, u32[]{:S(2)}) copy-start(bf16[1,1024]{1,0:T(2,128)(2,1)} %param.16) | copy-start | bytes 6148
  40.3 68.3 %all-to-all-start.1 = ((bf16[16,48,2048]{2,1,0:T(8,128)(2,1)}), bf16[16,48,2048]{2,1,0:T(8,128)(2,1)}, u32[]{:S(2)}, u32[]{:S(2)}) async-start(bf16[16,48,2048]{2,1,0:T(8,128)(2,1)} %bitcast.82), calls=%async_computation.1 | async-start | bytes 6291456 | tf_op jit(solution)/shard_map/all_to_all | solution.py:186
  47.3 12.7 %all-gather.5.cloned.1.call-start = ((), (), s32[]{:S(2)}) async-start(), calls=%async_computation.7 | async-start | bytes 1572864 | tf_op jit(solution)/shard_map/all_gather | solution.py:161
  108.6 76.9 %all-to-all-start = ((bf16[16,48,2048]{2,1,0:T(8,128)(2,1)}), bf16[16,48,2048]{2,1,0:T(8,128)(2,1)}, u32[]{:S(2)}, u32[]{:S(2)}) async-start(bf16[16,48,2048]{2,1,0:T(8,128)(2,1)} %bitcast.83), calls=%async_computation | async-start | bytes 6291456 | tf_op jit(solution)/shard_map/all_to_all | solution.py:193
  124.8 204.8 %reduce-scatter.2.cloned.1.call-start = ((), (), s32[]{:S(2)}) async-start(), calls=%async_computation.8 | async-start | bytes 4718592 | tf_op jit(solution)/shard_map/reduce_scatter | solution.py:225
  125.0 5.0 %copy-start.8 = (bf16[1,2048,512]{2,1,0:T(8,128)(2,1)S(1)}, bf16[1,2048,512]{2,1,0:T(8,128)(2,1)}, u32[]{:S(2)}) copy-start(bf16[1,2048,512]{2,1,0:T(8,128)(2,1)} %param.18) | copy-start | bytes 6291460
  185.5 5.5 %copy-start.10 = (f32[768,512]{0,1:T(8,128)S(1)}, f32[768,512]{0,1:T(8,128)}, u32[]{:S(2)}) copy-start(f32[768,512]{0,1:T(8,128)} %fusion.7) | copy-start | bytes 4718596
  185.5 5.6 %copy-start.14 = (f32[768,512]{0,1:T(8,128)S(1)}, f32[768,512]{0,1:T(8,128)}, u32[]{:S(2)}) copy-start(f32[768,512]{0,1:T(8,128)} %fusion.10) | copy-start | bytes 4718596
  191.1 2.4 copy-start.12
  191.1 2.3 copy-start.9
  280.1 0.8 copy-start.5
  280.1 2.9 copy-start.4
  280.2 4.4 copy-start.6
  289.4 11.2 %all-to-all-start.4 = ((bf16[16,1,48]{2,1,0:T(2,128)(2,1)}), bf16[16,1,48]{2,1,0:T(2,128)(2,1)S(1)}, u32[]{:S(2)}, u32[]{:S(2)}) async-start(bf16[16,1,48]{2,1,0:T(2,128)(2,1)} %all_to_all.28), calls=%async_computation.5 | async-start | bytes 16384 | tf_op jit(solution)/shard_map/all_to_all | solution.py:200
  303.9 20.4 %all-to-all-start.3 = ((f32[16,1,48]{2,1,0:T(1,128)}), f32[16,1,48]{2,1,0:T(1,128)S(1)}, u32[]{:S(2)}, u32[]{:S(2)}) async-start(f32[16,1,48]{2,1,0:T(1,128)} %psum.28), calls=%async_computation.4 | async-start | bytes 16384 | tf_op jit(solution)/shard_map/all_to_all | solution.py:222
  307.4 6.6 %copy-start.11 = (f32[768,512]{0,1:T(8,128)S(1)}, f32[768,512]{0,1:T(8,128)}, u32[]{:S(2)}) copy-start(f32[768,512]{0,1:T(8,128)} %fusion.7) | copy-start | bytes 4718596
  307.4 127.1 %all-reduce.3.cloned.1.call-start = ((), (), s32[]{:S(2)}) async-start(), calls=%async_computation.9 | async-start | bytes 131072 | tf_op jit(solution)/shard_map/psum | solution.py:122
  307.7 6.3 %copy-start.13 = (f32[768,512]{0,1:T(8,128)S(1)}, f32[768,512]{0,1:T(8,128)}, u32[]{:S(2)}) copy-start(f32[768,512]{0,1:T(8,128)} %copy-done.12) | copy-start | bytes 4718596
  307.7 6.3 %copy-start.15 = (f32[768,512]{0,1:T(8,128)S(1)}, f32[768,512]{0,1:T(8,128)}, u32[]{:S(2)}) copy-start(f32[768,512]{0,1:T(8,128)} %fusion.10) | copy-start | bytes 4718596
  324.3 4.0 copy-start.3
  336.6 1.6 copy-start.2
  338.2 97.7 %copy-start.1 = (bf16[1,2048,512]{2,1,0:T(8,128)(2,1)S(1)}, bf16[1,2048,512]{2,1,0:T(8,128)(2,1)}, u32[]{:S(2)}) copy-start(bf16[1,2048,512]{2,1,0:T(8,128)(2,1)} %param.17) | copy-start | bytes 6291460
Sparse Core Ops, SparseCore 0:
  9.5 11.7 all-gather.2
  49.6 10.2 all-gather.4
  280.3 9.3 reduce-scatter.1
  329.7 104.7 all-reduce.2
where the time goes:
time: 450 us; the launch traced here: 443 us
  waiting for transfers between devices  198 us (44%)
  blocking collectives  98.8 us (22%)
  local copies, waits for them, and re-layouts  45.6 us (10%)
  matrix products  40.5 us (9%)
  starting transfers between devices  31.2 us (7%)
  between operations  14.5 us (3%)
  other arithmetic  14.2 us (3%)
    psum x1, waiting for transfers between devices, finish_tokens(): lax.psum(jnp.einsum('td,te->de', normed_part, dlogit, precision=highest),...  89.7 us
    all_to_all x1, blocking collectives, per_device(): lax.all_to_all(sender_view(part_rows, groups), 'dp', split_axis=0, concat...  84.8 us
    all_to_all x1, waiting for transfers between devices, per_device(): lax.all_to_all(send_z.reshape(experts, capacity, entire_width), 'dp', spl...  50.6 us
    all_to_all x1, waiting for transfers between devices, per_device(): lax.all_to_all(send_x.reshape(experts, capacity, entire_width), 'dp', spl...  33.7 us
    all_to_all x1, starting transfers between devices, per_device(): lax.all_to_all(send_z.reshape(experts, capacity, entire_width), 'dp', spl...  16.2 us
    all_gather x1, waiting for transfers between devices, per_device(): lax.all_gather(cotangent, 'expert', axis=1, tiled=True)  9.55 us
  transfers between devices with their start and end apart: 8, of which 6 were waited for; matrix products, arithmetic and copies ran while one was open for 15% of the time, Pallas kernels for 0%

commit v1 on v0

v1 whole, which is shorter than its diff:
```python
import jax
import jax.numpy as jnp
from jax import lax
from jax.sharding import PartitionSpec as P

SEQ = 4096

norm_eps = 1e-06
HIGHEST = lax.Precision.HIGHEST
F32 = jnp.float32
BF16 = jnp.bfloat16


def slot_targets(routes, experts, capacity):
    flat_routes = routes.reshape(-1)
    expert_ids = jnp.arange(experts, dtype=jnp.int32)
    onehot = (flat_routes[:, None] == expert_ids[None, :]).astype(jnp.int32)
    rank_run = jnp.cumsum(onehot, axis=0) - 1
    slots = flat_routes * capacity + jnp.sum(onehot * rank_run, axis=1)
    return slots.reshape(routes.shape)


def pair_swap(value):
    return lax.ppermute(value, "expert", [(0, 1), (1, 0)])


def core_sum(value):
    if lax.axis_size("expert") == 2:
        return value + pair_swap(value)
    return lax.psum(value, "expert")


def whole_features(part):
    if lax.axis_size("expert") == 2:
        other = pair_swap(part)
        first = lax.axis_index("expert") == 0
        return jnp.concatenate(
            [jnp.where(first, part, other), jnp.where(first, other, part)], axis=-1
        )
    return lax.all_gather(part, "expert", axis=part.ndim - 1, tiled=True)


def scatter_features(value):
    if lax.axis_size("expert") == 2:
        half = value.shape[-1] // 2
        low, high = value[..., :half], value[..., half:]
        first = lax.axis_index("expert") == 0
        other = pair_swap(jnp.where(first, high, low))
        return jnp.where(first, low, high).astype(F32) + other.astype(F32)
    return lax.psum_scatter(
        value, "expert", scatter_dimension=value.ndim - 1, tiled=True
    ).astype(F32)


def dp_sum(value):
    size = lax.axis_size("dp")
    step = 1
    while step < size:
        if size % (2 * step):
            return lax.psum(value, "dp")
        step *= 2
    step = 1
    while step < size:
        value = value + lax.ppermute(value, "dp", [(i, i ^ step) for i in range(size)])
        step *= 2
    return value


def all_to_all(value):
    return lax.all_to_all(value, "dp", split_axis=0, concat_axis=0, tiled=True)


def owner_view(arrived, groups, local):
    shaped = arrived.reshape((groups, local) + arrived.shape[1:])
    shaped = jnp.swapaxes(shaped, 0, 1)
    return shaped.reshape((local, groups * arrived.shape[1]) + arrived.shape[2:])


def sender_view(outgoing, groups):
    local = outgoing.shape[0]
    capacity = outgoing.shape[1] // groups
    shaped = outgoing.reshape((local, groups, capacity) + outgoing.shape[2:])
    shaped = jnp.swapaxes(shaped, 0, 1)
    return shaped.reshape((groups * local, capacity) + outgoing.shape[2:])


def selected_row(table, sample_index):
    return lax.dynamic_slice_in_dim(table, sample_index, 1, 0).astype(F32)


def split_bf16(value):
    high = value.astype(BF16)
    low = (value - high.astype(F32)).astype(BF16)
    return high, low


def per_device(
    latents, cotangent, routes, router_w, mod_shift, mod_scale, mod_gate, gate_w, up_w, down_w
):
    tok_rows, width = latents.shape
    experts = router_w.shape[1]
    local = gate_w.shape[0]
    groups = lax.axis_size("dp")
    entire_width = width * lax.axis_size("expert")
    capacity = 3 * tok_rows // experts
    slot_count = experts * capacity
    sample_index = lax.axis_index("dp") * tok_rows // SEQ

    targets = slot_targets(routes, experts, capacity)
    slot_ids = jnp.arange(slot_count, dtype=jnp.int32)
    hit0 = targets[:, 0][None, :] == slot_ids[:, None]
    hit1 = targets[:, 1][None, :] == slot_ids[:, None]
    fill = (hit0 | hit1).astype(BF16)

    def to_slots(rows_b):
        rows = jnp.dot(fill, rows_b, preferred_element_type=F32).astype(BF16)
        return rows.reshape(experts, capacity, width)

    cot = cotangent.astype(F32)
    scaled_dy = (selected_row(mod_gate, sample_index) * cot).astype(BF16)
    got_z = all_to_all(to_slots(scaled_dy))

    x = latents.astype(F32)
    sums = jnp.stack([jnp.sum(x, axis=1), jnp.sum(x * x, axis=1)])
    mean, msq = core_sum(sums) / entire_width
    inv_std = lax.rsqrt(msq - mean * mean + norm_eps)[:, None]
    xhat = (x - mean[:, None]) * inv_std
    amp = 1.0 + selected_row(mod_scale, sample_index)
    normed = xhat * amp + selected_row(mod_shift, sample_index)
    got_x = all_to_all(to_slots(normed.astype(BF16)))

    logits = core_sum(lax.dot_general(
        router_w, normed, (((0,), (1,)), ((), ())), precision=HIGHEST
    )).T
    chances = jax.nn.sigmoid(logits)
    expert_ids = jnp.arange(experts, dtype=jnp.int32)
    hits = routes[:, :, None] == expert_ids[None, None, :]
    picked = jnp.sum(jnp.where(hits, chances[:, None, :], 0.0), axis=2)
    pick_sum = jnp.sum(picked, axis=1, keepdims=True)
    weights = picked / pick_sum
    w0, w1 = weights[:, 0], weights[:, 1]
    send_w = jnp.sum(
        jnp.where(hit0, w0[None, :], 0.0) + jnp.where(hit1, w1[None, :], 0.0), axis=1
    ).astype(BF16)
    got_w = all_to_all(send_w.reshape(experts, capacity))

    rows_z = owner_view(whole_features(got_z), groups, local)
    rows_x = owner_view(whole_features(got_x), groups, local)
    slot_w = owner_view(got_w, groups, local).astype(F32)[..., None]

    down_back = jnp.einsum("esd,ehd->esh", rows_z, down_w, preferred_element_type=F32)
    gate_lin = jnp.einsum("esd,edh->esh", rows_x, gate_w, preferred_element_type=F32)
    up_lin = jnp.einsum("esd,edh->esh", rows_x, up_w, preferred_element_type=F32)
    gate_sig = jax.nn.sigmoid(gate_lin)
    gate_act = gate_lin * gate_sig
    hidden = gate_act * up_lin
    slot_score = jnp.sum(hidden * down_back, axis=-1)
    d_gate = down_back * up_lin * gate_sig * (1.0 + gate_lin * (1.0 - gate_sig))
    d_up = down_back * gate_act
    part = (
        jnp.einsum("esh,edh->esd", d_gate.astype(BF16), gate_w, preferred_element_type=F32)
        + jnp.einsum("esh,edh->esd", d_up.astype(BF16), up_w, preferred_element_type=F32)
    ).astype(BF16)
    summed = scatter_features(part).astype(BF16)

    back_scores = all_to_all(sender_view(slot_score, groups)).reshape(-1)
    back_rows = all_to_all(sender_view(summed, groups)).reshape(slot_count, width)

    gate_wt = (slot_w * d_gate).astype(BF16)
    up_wt = (slot_w * d_up).astype(BF16)
    hidden_wt = (slot_w * hidden).astype(BF16)
    grad_gate = jnp.einsum("esd,esh->edh", rows_x, gate_wt, preferred_element_type=F32)
    grad_up = jnp.einsum("esd,esh->edh", rows_x, up_wt, preferred_element_type=F32)
    grad_down = jnp.einsum("esh,esd->ehd", hidden_wt, rows_z, preferred_element_type=F32)

    score_row = back_scores[:, None]
    score = core_sum(jnp.stack([
        jnp.sum(jnp.where(hit0, score_row, 0.0), axis=0),
        jnp.sum(jnp.where(hit1, score_row, 0.0), axis=0),
    ])).T
    mean_score = jnp.sum(weights * score, axis=1, keepdims=True)
    d_pick = (score - mean_score) / pick_sum * picked * (1.0 - picked)
    dlogit = jnp.sum(jnp.where(hits, d_pick[:, :, None], 0.0), axis=1)
    grad_router = dp_sum(lax.dot_general(
        dlogit, normed, (((0,), (0,)), ((), ())), precision=HIGHEST
    )).T

    mix = jnp.where(hit0, w0[None, :], 0.0) + jnp.where(hit1, w1[None, :], 0.0)
    mix_high, mix_low = split_bf16(mix)
    contract = (((0,), (0,)), ((), ()))
    combined = lax.dot_general(
        mix_high, back_rows, contract, preferred_element_type=F32
    ) + lax.dot_general(mix_low, back_rows, contract, preferred_element_type=F32)
    dnormed = combined + lax.dot_general(
        dlogit, router_w, (((1,), (1,)), ((), ())), precision=HIGHEST
    )
    dxhat = dnormed * amp
    m_one, m_two = core_sum(
        jnp.stack([jnp.sum(dxhat, axis=1), jnp.sum(dxhat * xhat, axis=1)])
    ) / entire_width
    latent_gradient = inv_std * (dxhat - m_one[:, None] - xhat * m_two[:, None]) + cot
    return (
        latent_gradient.astype(BF16),
        grad_gate.astype(BF16),
        grad_up.astype(BF16),
        grad_down.astype(BF16),
        grad_router,
    )


def solution(mesh):
    placed = (
        P("dp", "expert"),
        P("dp", "expert"),
        P("dp", None),
        P("expert", None),
        P(None, "expert"),
        P(None, "expert"),
        P(None, "expert"),
        P("dp", None, "expert"),
        P("dp", None, "expert"),
        P("dp", "expert", None),
    )
    return jax.shard_map(
        per_device,
        mesh=mesh,
        in_specs=placed,
        out_specs=(
            P("dp", "expert"),
            P("dp", None, "expert"),
            P("dp", None, "expert"),
            P("dp", "expert", None),
            P("expert", None),
        ),
        check_vma=False,
    )
```

time: 450 us -> 198 us (0.44)
  the two profiles are of different devices: /device:TPU:0 before, /device:TPU:13 now
where the time goes in v1:
time: 198 us; the launch traced here: 197 us
  waiting for transfers between devices  95.3 us (48%)
  starting transfers between devices  41.2 us (21%)
  matrix products  35.7 us (18%)
  other arithmetic  15.9 us (8%)
  local copies, waits for them, and re-layouts  8.22 us (4%)
    all_to_all x5, waiting for transfers between devices, all_to_all(): return lax.all_to_all(value, 'dp', split_axis=0, concat_axis=0, tiled=True)  81.9 us
    all_to_all x5, starting transfers between devices, all_to_all(): return lax.all_to_all(value, 'dp', split_axis=0, concat_axis=0, tiled=True)  26.7 us
    ppermute x7, starting transfers between devices, pair_swap(): return lax.ppermute(value, 'expert', [(0, 1), (1, 0)])  9.8 us
    ppermute x7, waiting for transfers between devices, pair_swap(): return lax.ppermute(value, 'expert', [(0, 1), (1, 0)])  7.28 us
    dot_general x1, matrix products, per_device(): jnp.einsum('esd,esh->edh', rows_x, gate_wt, preferred_element_type=F32)  6.77 us
    ppermute x4, waiting for transfers between devices, dp_sum(): lax.ppermute(value, 'dp', [(i, i ^ step) for i in range(size)])  6.17 us
    unnamed x41, local copies, waits for them, and re-layouts  5.44 us
    ppermute x4, starting transfers between devices, dp_sum(): lax.ppermute(value, 'dp', [(i, i ^ step) for i in range(size)])  4.79 us
  transfers between devices with their start and end apart: 16, of which 11 were waited for; matrix products, arithmetic and copies ran while one was open for 16% of the time, Pallas kernels for 0%

profile of v1, /device:TPU:13, one launch (start us, length us, event | category | flops | bytes accessed | tf_op | source)
XLA Modules:
  0.0 197.5 jit_solution(15690160221689917427)
XLA Ops:
  0.6 1.0 copy.48
  1.6 0.1 eq.77
  1.9 0.7 mul.176
  2.6 1.2 reduce-window.6
  3.8 0.2 slice_reduce_fusion
  4.1 0.1 reduce_sum.122
  4.3 0.7 multiply_add_fusion
  5.1 2.8 %convolution_convert_fusion.4 = bf16[768,1024]{1,0:T(8,128)(2,1)} fusion(bf16[256,1024]{1,0:T(8,128)(2,1)} %param.11, f32[1024]{0:T(1024)S(1)} %bitcast.124, s32[256]{0:T(256)S(1)} %bitcast.130, s32[256]{0:T(256)S(1)} %bitcast.125), kind=kOutput, calls=%fused_computation.21 | convolution fusion | flops 404815872 | bytes 2103296 | tf_op jit(solution)/shard_map/dot_general | solution.py:116
  7.9 6.7 %all-to-all-start = ((bf16[16,48,1024]{2,1,0:T(8,128)(2,1)}), bf16[16,48,1024]{2,1,0:T(8,128)(2,1)}, u32[]{:S(2)}, u32[]{:S(2)}) async-start(bf16[16,48,1024]{2,1,0:T(8,128)(2,1)} %bitcast.93), calls=%async_computation | async-start | bytes 3145728 | tf_op jit(solution)/shard_map/all_to_all | solution.py:70
  14.6 0.2 convert_reduce_fusion
  14.9 1.3 collective-permute-start
  16.2 0.8 collective-permute-done
  17.0 1.9 convolution_convert_fusion.3
  18.9 32.8 %all-to-all-done = bf16[16,48,1024]{2,1,0:T(8,128)(2,1)} async-done(((bf16[16,48,1024]{2,1,0:T(8,128)(2,1)}), bf16[16,48,1024]{2,1,0:T(8,128)(2,1)}, u32[]{:S(2)}, u32[]{:S(2)}) %all-to-all-start) | async-done | bytes 1572896 | tf_op jit(solution)/shard_map/all_to_all | solution.py:70
  51.7 4.5 %all-to-all-start.1 = ((bf16[16,48,1024]{2,1,0:T(8,128)(2,1)}), bf16[16,48,1024]{2,1,0:T(8,128)(2,1)}, u32[]{:S(2)}, u32[]{:S(2)}) async-start(bf16[16,48,1024]{2,1,0:T(8,128)(2,1)} %bitcast.94), calls=%async_computation.1 | async-start | bytes 3145728 | tf_op jit(solution)/shard_map/all_to_all | solution.py:70
  56.2 1.7 collective-permute-start.2
  57.8 35.2 %all-to-all-done.1 = bf16[16,48,1024]{2,1,0:T(8,128)(2,1)} async-done(((bf16[16,48,1024]{2,1,0:T(8,128)(2,1)}), bf16[16,48,1024]{2,1,0:T(8,128)(2,1)}, u32[]{:S(2)}, u32[]{:S(2)}) %all-to-all-start.1) | async-done | bytes 1572896 | tf_op jit(solution)/shard_map/all_to_all | solution.py:70
  93.1 1.4 collective-permute-start.3
  94.5 3.4 %collective-permute-done.3 = bf16[16,48,1024]{2,1,0:T(8,128)(2,1)} collective-permute-done((bf16[16,48,1024]{2,1,0:T(8,128)(2,1)}, bf16[16,48,1024]{2,1,0:T(8,128)(2,1)}, u32[]{:S(2)}, u32[]{:S(2)}) %collective-permute-start.3) | collective-permute-done | bytes 1572896 | tf_op jit(solution)/shard_map/ppermute | solution.py:24
  97.8 3.2 %broadcast_select_fusion.1 = (bf16[16,48,1024]{2,1,0:T(8,128)(2,1)S(1)}, bf16[16,48,1024]{2,1,0:T(8,128)(2,1)S(1)}, bf16[16,48,1024]{2,1,0:T(8,128)(2,1)S(1)}, bf16[16,48,1024]{2,1,0:T(8,128)(2,1)S(1)}) fusion(bf16[16,48,1024]{2,1,0:T(8,128)(2,1)} %all-to-all-done.1, bf16[16,48,1024]{2,1,0:T(8,128)(2,1)} %collective-permute-done.3, pred[]{:T(512)S(6)} %eq.92, ...), kind=kLoop, calls=%fused_computation.33 | loop fusion | flops 3145728 | bytes 12582913 | tf_op jit(solution)/shard_map/jit(_where)/select_n | solution.py:38
  101.1 0.2 pad_maximum_fusion.1
  101.3 2.0 fusion.6
  103.3 0.7 copy-done.7
  104.1 2.0 %fusion.9 = f32[768,512]{0,1:T(8,128)S(1)} fusion(bf16[768,2048]{1,0:T(8,128)(2,1)S(1)} %bitcast.90, bf16[1,2048,512]{2,1,0:T(8,128)(2,1)S(1)} %copy-done.7), kind=kOutput, calls=%fused_computation.16 | convolution fusion | flops 1610612736 | bytes 6815744 | tf_op jit(solution)/shard_map/esd,edh->esh/dot_general | solution.py:153
  106.1 0.2 pad_maximum_fusion
  106.3 2.9 %copy-done.17 = bf16[1,512,2048]{2,1,0:T(8,128)(2,1)S(1)} copy-done((bf16[1,512,2048]{2,1,0:T(8,128)(2,1)S(1)}, bf16[1,512,2048]{2,1,0:T(8,128)(2,1)}, u32[]{:S(2)}) %copy-start.17) | copy-done | bytes 2097176
  109.2 2.0 %multiply_reduce_fusion = (f32[768]{0:T(1024)S(1)}, f32[768,512]{0,1:T(8,128)S(1)}) fusion(f32[768,512]{0,1:T(8,128)S(1)} %fusion.9, f32[768,512]{0,1:T(8,128)S(1)} %fusion.6, bf16[768,2048]{1,0:T(8,128)(2,1)S(1)} %bitcast.87, bf16[1,512,2048]{2,1,0:T(8,128)(2,1)S(1)} %copy-done.17), kind=kOutput, calls=%fused_computation.25 | convolution fusion | flops 1613364480 | bytes 9964544 | tf_op jit(solution)/shard_map/esd,ehd->esh/dot_general | solution.py:151
  111.3 2.4 %fusion.4 = f32[768,2048]{1,0:T(8,128)S(1)} fusion(bf16[1,2048,512]{2,1,0:T(8,128)(2,1)S(1)} %copy-done, f32[768,512]{0,1:T(8,128)S(1)} %fusion.6, f32[768,512]{0,1:T(8,128)S(1)} %get-tuple-element.27, f32[768,512]{0,1:T(8,128)S(1)} %fusion.9), kind=kOutput, calls=%fused_computation.11 | convolution fusion | flops 1614544896 | bytes 13107200 | tf_op jit(solution)/shard_map/esh,edh->esd/dot_general | solution.py:161
  113.7 1.9 fusion
  115.7 1.4 broadcast_select_fusion.4
  117.1 0.7 copy-done.1
  117.8 0.4 collective-permute-start.4
  118.2 1.1 convolution_bitcast_fusion
  119.3 0.2 collective-permute-start.1
  119.5 2.1 %collective-permute-done.1 = f32[16,256]{1,0:T(8,128)S(1)} collective-permute-done((f32[16,256]{1,0:T(8,128)S(1)}, f32[16,256]{1,0:T(8,128)S(1)}, u32[]{:S(2)}, u32[]{:S(2)}) %collective-permute-start.1) | collective-permute-done | bytes 16416 | tf_op jit(solution)/shard_map/ppermute | solution.py:24
  121.7 0.7 all_to_all.22
  122.3 3.7 %all-to-all-start.3 = ((f32[16,1,48]{2,1,0:T(1,128)}), f32[16,1,48]{2,1,0:T(1,128)S(1)}, u32[]{:S(2)}, u32[]{:S(2)}) async-start(f32[16,1,48]{2,1,0:T(1,128)} %all_to_all.22), calls=%async_computation.3 | async-start | bytes 16384 | tf_op jit(solution)/shard_map/all_to_all | solution.py:70
  126.0 4.1 %all-to-all-done.3 = f32[16,1,48]{2,1,0:T(1,128)S(1)} async-done(((f32[16,1,48]{2,1,0:T(1,128)}), f32[16,1,48]{2,1,0:T(1,128)S(1)}, u32[]{:S(2)}, u32[]{:S(2)}) %all-to-all-start.3) | async-done | bytes 3104 | tf_op jit(solution)/shard_map/all_to_all | solution.py:70
  130.1 0.5 broadcast.93
  130.6 0.7 reduce.12
  131.4 0.6 select_reduce_fusion.1
  132.0 0.7 convert_element_type.153
  132.7 5.4 %all-to-all-start.4 = ((bf16[16,1,48]{2,1,0:T(2,128)(2,1)}), bf16[16,1,48]{2,1,0:T(2,128)(2,1)S(1)}, u32[]{:S(2)}, u32[]{:S(2)}) async-start(bf16[16,1,48]{2,1,0:T(2,128)(2,1)} %convert_element_type.153), calls=%async_computation.4 | async-start | bytes 16384 | tf_op jit(solution)/shard_map/all_to_all | solution.py:70
  138.0 4.5 %add_convert_fusion.1 = bf16[1,768,1024]{2,1,0:T(8,128)(2,1)} fusion(bf16[1,768,1024]{2,1,0:T(8,128)(2,1)} %collective-permute-done.4, pred[]{:T(512)S(6)} %eq.92, bf16[1,768,2048]{2,1,0:T(8,128)(2,1)} %copy-done.1), kind=kLoop, calls=%fused_computation.3 | loop fusion | flops 3932160 | bytes 6291457 | tf_op jit(solution)/shard_map/convert_element_type | solution.py:164
  142.6 6.4 %all-to-all-start.2 = ((bf16[16,48,1024]{2,1,0:T(8,128)(2,1)}), bf16[16,48,1024]{2,1,0:T(8,128)(2,1)}, u32[]{:S(2)}, u32[]{:S(2)}) async-start(bf16[16,48,1024]{2,1,0:T(8,128)(2,1)} %bitcast.86), calls=%async_computation.2 | async-start | bytes 3145728 | tf_op jit(solution)/shard_map/all_to_all | solution.py:70
  149.0 2.7 %collective-permute-start.5 = (f32[2,256]{1,0:T(2,128)S(1)}, f32[2,256]{1,0:T(2,128)S(1)}, u32[]{:S(2)}, u32[]{:S(2)}) collective-permute-start(f32[2,256]{1,0:T(2,128)S(1)} %pad_maximum_fusion.3), channel_id=1, source_target_pairs={{0,1},{1,0},{2,3},{3,2},{4,5},{5,4},{6,7},{7,6},{8,9},{9,8},{10,11... | collective-permute-start | bytes 6152 | tf_op jit(solution)/shard_map/ppermute | solution.py:24
  151.7 0.8 collective-permute-done.5
  152.6 0.8 fusion.23
  153.4 1.2 collective-permute-start.7
  154.8 6.8 %fusion.1 = bf16[1,2048,512]{2,1,0:T(8,128)(2,1)} fusion(bf16[768,2048]{1,0:T(8,128)(2,1)} %bitcast.91, f32[768]{0:T(1024)S(1)} %reshape.183, f32[768,512]{0,1:T(8,128)} %copy-done.8, f32[768,512]{0,1:T(8,128)} %copy-done.10, f32[768,512]{0,1:T(8,128)} %copy-done.18), kind=kOutput, calls=%fused_computation.8 | convolution fusion | flops 1615986688 | bytes 9964544 | tf_op jit(solution)/shard_map/esd,esh->edh/dot_general | solution.py:172
  161.6 0.3 collective-permute-start.8
  161.9 3.3 %fusion.2 = bf16[1,2048,512]{2,1,0:T(8,128)(2,1)} fusion(bf16[768,2048]{1,0:T(8,128)(2,1)S(1)} %bitcast.92, f32[768]{0:T(1024)S(1)} %reshape.183, f32[768,512]{0,1:T(8,128)S(1)} %copy-done.11, f32[768,512]{0,1:T(8,128)S(1)} %copy-done.9), kind=kOutput, calls=%fused_computation.9 | convolution fusion | flops 1614413824 | bytes 8391680 | tf_op jit(solution)/shard_map/esd,esh->edh/dot_general | solution.py:173
  165.3 0.6 collective-permute-done.8
  166.0 3.2 %fusion.3 = bf16[1,512,2048]{2,1,0:T(8,128)(2,1)} fusion(bf16[768,2048]{1,0:T(8,128)(2,1)S(1)} %bitcast.88, f32[768]{0:T(1024)S(1)} %reshape.183, f32[768,512]{0,1:T(8,128)S(1)} %copy-done.19, f32[768,512]{0,1:T(8,128)S(1)} %copy-done.9), kind=kOutput, calls=%fused_computation.10 | convolution fusion | flops 1614413824 | bytes 8391680 | tf_op jit(solution)/shard_map/esh,esd->ehd/dot_general | solution.py:174
  169.2 5.5 %collective-permute-done.9 = f32[16,1024]{1,0:T(8,128)S(1)} collective-permute-done((f32[16,1024]{1,0:T(8,128)S(1)}, f32[16,1024]{1,0:T(8,128)S(1)}, u32[]{:S(2)}, u32[]{:S(2)}) %collective-permute-start.9) | collective-permute-done | bytes 65568 | tf_op jit(solution)/shard_map/ppermute | solution.py:64
  174.8 3.1 %collective-permute-start.10 = (f32[16,1024]{1,0:T(8,128)S(1)}, f32[16,1024]{1,0:T(8,128)S(1)}, u32[]{:S(2)}, u32[]{:S(2)}) collective-permute-start(f32[16,1024]{1,0:T(8,128)S(1)} %add.120), channel_id=1, source_target_pairs={{0,16},{2,18},{4,20},{6,22},{8,24},{10,26},{12,28},{14,30},{16,0},... | collective-permute-start | bytes 196616 | tf_op jit(solution)/shard_map/ppermute | solution.py:64
  177.9 9.8 %all-to-all-done.2 = bf16[16,48,1024]{2,1,0:T(8,128)(2,1)} async-done(((bf16[16,48,1024]{2,1,0:T(8,128)(2,1)}), bf16[16,48,1024]{2,1,0:T(8,128)(2,1)}, u32[]{:S(2)}, u32[]{:S(2)}) %all-to-all-start.2) | async-done | bytes 1572896 | tf_op jit(solution)/shard_map/all_to_all | solution.py:70
  187.7 2.1 %fusion.58 = f32[256,1024]{1,0:T(8,128)S(1)} fusion(bf16[768,1024]{1,0:T(8,128)(2,1)} %bitcast.23, f32[256]{0:T(256)S(1)} %bitcast.139, s32[256]{0:T(256)S(1)} %bitcast.133, f32[256]{0:T(256)S(1)} %bitcast.136, s32[256]{0:T(256)S(1)} %bitcast.128), kind=kOutput, calls=%fused_computation.86 | convolution fusion | flops 404422656 | bytes 2625536 | tf_op jit(solution)/shard_map/dot_general | solution.py:193
  189.8 2.0 %convolution_add_fusion.1 = f32[256,1024]{1,0:T(8,128)S(1)} fusion(f32[256,1024]{1,0:T(8,128)S(1)} %fusion.58, bf16[768,1024]{1,0:T(8,128)(2,1)} %bitcast.23, f32[256]{0:T(256)S(1)} %bitcast.140, s32[256]{0:T(256)S(1)} %bitcast.134, f32[256]{0:T(256)S(1)} %bitcast.137, s32[256]{0:T(256)S(1)} %bitcast.129), kind=kOutput, calls=%fused_computation.39 | convolution fusion | flops 404094976 | bytes 3674112 | tf_op jit(solution)/shard_map/dot_general | solution.py:191
  191.8 1.4 fusion.80
  193.2 2.2 %collective-permute-start.6 = (f32[2,256]{1,0:T(2,128)S(1)}, f32[2,256]{1,0:T(2,128)S(1)}, u32[]{:S(2)}, u32[]{:S(2)}) collective-permute-start(f32[2,256]{1,0:T(2,128)S(1)} %pad_maximum_fusion.4), channel_id=1, source_target_pairs={{0,1},{1,0},{2,3},{3,2},{4,5},{5,4},{6,7},{7,6},{8,9},{9,8},{10,11... | collective-permute-start | bytes 6152 | tf_op jit(solution)/shard_map/ppermute | solution.py:24
  195.4 0.6 add_bitcast_fusion
  196.0 0.2 collective-permute-done.6
  196.2 1.2 fusion.16
  (73 shorter events, 0.9 us)
Async XLA Ops:
  0.6 100.7 %copy-start = (bf16[1,2048,512]{2,1,0:T(8,128)(2,1)S(1)}, bf16[1,2048,512]{2,1,0:T(8,128)(2,1)}, u32[]{:S(2)}) copy-start(bf16[1,2048,512]{2,1,0:T(8,128)(2,1)} %param.17) | copy-start | bytes 6291460
  7.8 6.7 %copy-start.2 = (bf16[256,1024]{1,0:T(8,128)(2,1)S(1)}, bf16[256,1024]{1,0:T(8,128)(2,1)}, u32[]{:S(2)}) copy-start(bf16[256,1024]{1,0:T(8,128)(2,1)} %param.10) | copy-start | bytes 1572868
  7.8 8.3 %copy-start.15 = (bf16[1,1024]{1,0:T(2,128)(2,1)S(1)}, bf16[1,1024]{1,0:T(2,128)(2,1)}, u32[]{:S(2)}) copy-start(bf16[1,1024]{1,0:T(2,128)(2,1)} %param.15) | copy-start | bytes 6148
  7.8 8.3 %copy-start.16 = (bf16[1,1024]{1,0:T(2,128)(2,1)S(1)}, bf16[1,1024]{1,0:T(2,128)(2,1)}, u32[]{:S(2)}) copy-start(bf16[1,1024]{1,0:T(2,128)(2,1)} %param.14) | copy-start | bytes 6148
  7.9 43.8 %all-to-all-start = ((bf16[16,48,1024]{2,1,0:T(8,128)(2,1)}), bf16[16,48,1024]{2,1,0:T(8,128)(2,1)}, u32[]{:S(2)}, u32[]{:S(2)}) async-start(bf16[16,48,1024]{2,1,0:T(8,128)(2,1)} %bitcast.93), calls=%async_computation | async-start | bytes 3145728 | tf_op jit(solution)/shard_map/all_to_all | solution.py:70
  14.9 2.1 %collective-permute-start = (f32[2,256]{1,0:T(2,128)S(1)}, f32[2,256]{1,0:T(2,128)S(1)}, u32[]{:S(2)}, u32[]{:S(2)}) collective-permute-start(f32[2,256]{1,0:T(2,128)S(1)} %pad_maximum_fusion.2), channel_id=1, source_target_pairs={{0,1},{1,0},{2,3},{3,2},{4,5},{5,4},{6,7},{7,6},{8,9},{9,8},{10,11... | collective-permute-start | bytes 6152 | tf_op jit(solution)/shard_map/ppermute | solution.py:24
  51.7 41.4 %all-to-all-start.1 = ((bf16[16,48,1024]{2,1,0:T(8,128)(2,1)}), bf16[16,48,1024]{2,1,0:T(8,128)(2,1)}, u32[]{:S(2)}, u32[]{:S(2)}) async-start(bf16[16,48,1024]{2,1,0:T(8,128)(2,1)} %bitcast.94), calls=%async_computation.1 | async-start | bytes 3145728 | tf_op jit(solution)/shard_map/all_to_all | solution.py:70
  56.2 38.3 %collective-permute-start.2 = (bf16[16,48,1024]{2,1,0:T(8,128)(2,1)}, bf16[16,48,1024]{2,1,0:T(8,128)(2,1)}, u32[]{:S(2)}, u32[]{:S(2)}) collective-permute-start(bf16[16,48,1024]{2,1,0:T(8,128)(2,1)} %all-to-all-done), channel_id=1, source_target_pairs={{0,1},{1,0},{2,3},{3,2},{4,5},{5,4},{6,7},{7,6},{8,9},{9,8},{10,11... | collective-permute-start | bytes 4718600 | tf_op jit(solution)/shard_map/ppermute | solution.py:24
  93.1 4.8 %collective-permute-start.3 = (bf16[16,48,1024]{2,1,0:T(8,128)(2,1)}, bf16[16,48,1024]{2,1,0:T(8,128)(2,1)}, u32[]{:S(2)}, u32[]{:S(2)}) collective-permute-start(bf16[16,48,1024]{2,1,0:T(8,128)(2,1)} %all-to-all-done.1), channel_id=1, source_target_pairs={{0,1},{1,0},{2,3},{3,2},{4,5},{5,4},{6,7},{7,6},{8,9},{9,8},{10,11... | collective-permute-start | bytes 4718600 | tf_op jit(solution)/shard_map/ppermute | solution.py:24
  101.3 2.0 %copy-start.5 = (bf16[16,48,2048]{2,1,0:T(8,128)(2,1)}, bf16[16,48,2048]{2,1,0:T(8,128)(2,1)S(1)}, u32[]{:S(2)}) copy-start(bf16[16,48,2048]{2,1,0:T(8,128)(2,1)S(1)} %pad_maximum_fusion.1) | copy-start | bytes 9437188
  101.3 2.7 %copy-start.7 = (bf16[1,2048,512]{2,1,0:T(8,128)(2,1)S(1)}, bf16[1,2048,512]{2,1,0:T(8,128)(2,1)}, u32[]{:S(2)}) copy-start(bf16[1,2048,512]{2,1,0:T(8,128)(2,1)} %param.18) | copy-start | bytes 6291460
  104.1 9.6 %copy-start.8 = (f32[768,512]{0,1:T(8,128)}, f32[768,512]{0,1:T(8,128)S(1)}, u32[]{:S(2)}) copy-start(f32[768,512]{0,1:T(8,128)S(1)} %fusion.6) | copy-start | bytes 4718596
  106.1 5.2 %copy-start.18 = (f32[768,512]{0,1:T(8,128)}, f32[768,512]{0,1:T(8,128)S(1)}, u32[]{:S(2)}) copy-start(f32[768,512]{0,1:T(8,128)S(1)} %fusion.9) | copy-start | bytes 4718596
  106.1 3.2 %copy-start.17 = (bf16[1,512,2048]{2,1,0:T(8,128)(2,1)S(1)}, bf16[1,512,2048]{2,1,0:T(8,128)(2,1)}, u32[]{:S(2)}) copy-start(bf16[1,512,2048]{2,1,0:T(8,128)(2,1)} %param.19) | copy-start | bytes 6291460
  106.3 5.0 %copy-start.3 = (bf16[16,48,2048]{2,1,0:T(8,128)(2,1)}, bf16[16,48,2048]{2,1,0:T(8,128)(2,1)S(1)}, u32[]{:S(2)}) copy-start(bf16[16,48,2048]{2,1,0:T(8,128)(2,1)S(1)} %pad_maximum_fusion) | copy-start | bytes 9437188
  111.3 2.4 %copy-start.10 = (f32[768,512]{0,1:T(8,128)}, f32[768,512]{0,1:T(8,128)S(1)}, u32[]{:S(2)}) copy-start(f32[768,512]{0,1:T(8,128)S(1)} %get-tuple-element.27) | copy-start | bytes 4718596
  115.6 2.2 %copy-start.1 = (bf16[1,768,2048]{2,1,0:T(8,128)(2,1)}, bf16[1,768,2048]{2,1,0:T(8,128)(2,1)S(1)}, u32[]{:S(2)}) copy-start(bf16[1,768,2048]{2,1,0:T(8,128)(2,1)S(1)} %fusion) | copy-start | bytes 9437188
  115.6 2.6 %copy-start.13 = (f32[1024,16]{0,1:T(8,128)S(1)}, f32[1024,16]{0,1:T(8,128)}, u32[]{:S(2)}) copy-start(f32[1024,16]{0,1:T(8,128)} %param.13) | copy-start | bytes 196612
  115.7 6.0 %copy-start.14 = (s32[256,2]{0,1:T(2,128)S(1)}, s32[256,2]{0,1:T(2,128)}, u32[]{:S(2)}) copy-start(s32[256,2]{0,1:T(2,128)} %param.12) | copy-start | bytes 6148
  117.8 20.2 %collective-permute-start.4 = (bf16[1,768,1024]{2,1,0:T(8,128)(2,1)}, bf16[1,768,1024]{2,1,0:T(8,128)(2,1)}, u32[]{:S(2)}, u32[]{:S(2)}) collective-permute-start(bf16[1,768,1024]{2,1,0:T(8,128)(2,1)} %broadcast_select_fusion.4), channel_id=1, source_target_pairs={{0,1},{1,0},{2,3},{3,2},{4,5},{5,4},{6,7},{7,6},{8,9},{9,8},{10,11... | collective-permute-start | bytes 4718600 | tf_op jit(solution)/shard_map/ppermute | solution.py:24
  119.3 2.3 %collective-permute-start.1 = (f32[16,256]{1,0:T(8,128)S(1)}, f32[16,256]{1,0:T(8,128)S(1)}, u32[]{:S(2)}, u32[]{:S(2)}) collective-permute-start(f32[16,256]{1,0:T(8,128)S(1)} %convolution_bitcast_fusion), channel_id=1, source_target_pairs={{0,1},{1,0},{2,3},{3,2},{4,5},{5,4},{6,7},{7,6},{8,9},{9,8},{10,11... | collective-permute-start | bytes 49160 | tf_op jit(solution)/shard_map/ppermute | solution.py:24
  122.3 7.8 %all-to-all-start.3 = ((f32[16,1,48]{2,1,0:T(1,128)}), f32[16,1,48]{2,1,0:T(1,128)S(1)}, u32[]{:S(2)}, u32[]{:S(2)}) async-start(f32[16,1,48]{2,1,0:T(1,128)} %all_to_all.22), calls=%async_computation.3 | async-start | bytes 16384 | tf_op jit(solution)/shard_map/all_to_all | solution.py:70
  132.7 9.9 %all-to-all-start.4 = ((bf16[16,1,48]{2,1,0:T(2,128)(2,1)}), bf16[16,1,48]{2,1,0:T(2,128)(2,1)S(1)}, u32[]{:S(2)}, u32[]{:S(2)}) async-start(bf16[16,1,48]{2,1,0:T(2,128)(2,1)} %convert_element_type.153), calls=%async_computation.4 | async-start | bytes 16384 | tf_op jit(solution)/shard_map/all_to_all | solution.py:70
  142.6 45.1 %all-to-all-start.2 = ((bf16[16,48,1024]{2,1,0:T(8,128)(2,1)}), bf16[16,48,1024]{2,1,0:T(8,128)(2,1)}, u32[]{:S(2)}, u32[]{:S(2)}) async-start(bf16[16,48,1024]{2,1,0:T(8,128)(2,1)} %bitcast.86), calls=%async_computation.2 | async-start | bytes 3145728 | tf_op jit(solution)/shard_map/all_to_all | solution.py:70
  149.0 3.5 %collective-permute-start.5 = (f32[2,256]{1,0:T(2,128)S(1)}, f32[2,256]{1,0:T(2,128)S(1)}, u32[]{:S(2)}, u32[]{:S(2)}) collective-permute-start(f32[2,256]{1,0:T(2,128)S(1)} %pad_maximum_fusion.3), channel_id=1, source_target_pairs={{0,1},{1,0},{2,3},{3,2},{4,5},{5,4},{6,7},{7,6},{8,9},{9,8},{10,11... | collective-permute-start | bytes 6152 | tf_op jit(solution)/shard_map/ppermute | solution.py:24
  153.4 8.1 %collective-permute-start.7 = (f32[16,1024]{1,0:T(8,128)S(1)}, f32[16,1024]{1,0:T(8,128)S(1)}, u32[]{:S(2)}, u32[]{:S(2)}) collective-permute-start(f32[16,1024]{1,0:T(8,128)S(1)} %fusion.23), channel_id=1, source_target_pairs={{0,2},{2,0},{4,6},{6,4},{8,10},{10,8},{12,14},{14,12},{16,18},{18,... | collective-permute-start | bytes 196616 | tf_op jit(solution)/shard_map/ppermute | solution.py:64
  154.8 7.2 %copy-start.6 = (bf16[16,48,2048]{2,1,0:T(8,128)(2,1)S(1)}, bf16[16,48,2048]{2,1,0:T(8,128)(2,1)}, u32[]{:S(2)}) copy-start(bf16[16,48,2048]{2,1,0:T(8,128)(2,1)} %copy-done.5) | copy-start | bytes 9437188
  154.8 7.2 %copy-start.9 = (f32[768,512]{0,1:T(8,128)S(1)}, f32[768,512]{0,1:T(8,128)}, u32[]{:S(2)}) copy-start(f32[768,512]{0,1:T(8,128)} %copy-done.8) | copy-start | bytes 4718596
  154.8 7.2 %copy-start.11 = (f32[768,512]{0,1:T(8,128)S(1)}, f32[768,512]{0,1:T(8,128)}, u32[]{:S(2)}) copy-start(f32[768,512]{0,1:T(8,128)} %copy-done.10) | copy-start | bytes 4718596
  161.6 4.4 %copy-start.4 = (bf16[16,48,2048]{2,1,0:T(8,128)(2,1)S(1)}, bf16[16,48,2048]{2,1,0:T(8,128)(2,1)}, u32[]{:S(2)}) copy-start(bf16[16,48,2048]{2,1,0:T(8,128)(2,1)} %copy-done.3) | copy-start | bytes 9437188
  161.6 4.4 %copy-start.19 = (f32[768,512]{0,1:T(8,128)S(1)}, f32[768,512]{0,1:T(8,128)}, u32[]{:S(2)}) copy-start(f32[768,512]{0,1:T(8,128)} %copy-done.18) | copy-start | bytes 4718596
  161.6 4.3 %collective-permute-start.8 = (f32[16,1024]{1,0:T(8,128)S(1)}, f32[16,1024]{1,0:T(8,128)S(1)}, u32[]{:S(2)}, u32[]{:S(2)}) collective-permute-start(f32[16,1024]{1,0:T(8,128)S(1)} %add.118), channel_id=1, source_target_pairs={{0,4},{2,6},{4,0},{6,2},{8,12},{10,14},{12,8},{14,10},{16,20},{18,... | collective-permute-start | bytes 196616 | tf_op jit(solution)/shard_map/ppermute | solution.py:64
  165.9 8.8 %collective-permute-start.9 = (f32[16,1024]{1,0:T(8,128)S(1)}, f32[16,1024]{1,0:T(8,128)S(1)}, u32[]{:S(2)}, u32[]{:S(2)}) collective-permute-start(f32[16,1024]{1,0:T(8,128)S(1)} %add.119), channel_id=1, source_target_pairs={{0,8},{2,10},{4,12},{6,14},{8,0},{10,2},{12,4},{14,6},{16,24},{18,... | collective-permute-start | bytes 196616 | tf_op jit(solution)/shard_map/ppermute | solution.py:64
  174.8 20.6 %collective-permute-start.10 = (f32[16,1024]{1,0:T(8,128)S(1)}, f32[16,1024]{1,0:T(8,128)S(1)}, u32[]{:S(2)}, u32[]{:S(2)}) collective-permute-start(f32[16,1024]{1,0:T(8,128)S(1)} %add.120), channel_id=1, source_target_pairs={{0,16},{2,18},{4,20},{6,22},{8,24},{10,26},{12,28},{14,30},{16,0},... | collective-permute-start | bytes 196616 | tf_op jit(solution)/shard_map/ppermute | solution.py:64
  191.8 4.4 %copy-start.12 = (bf16[256,1024]{1,0:T(8,128)(2,1)S(1)}, bf16[256,1024]{1,0:T(8,128)(2,1)}, u32[]{:S(2)}) copy-start(bf16[256,1024]{1,0:T(8,128)(2,1)} %param.11) | copy-start | bytes 1572868
  193.2 3.0 %collective-permute-start.6 = (f32[2,256]{1,0:T(2,128)S(1)}, f32[2,256]{1,0:T(2,128)S(1)}, u32[]{:S(2)}, u32[]{:S(2)}) collective-permute-start(f32[2,256]{1,0:T(2,128)S(1)} %pad_maximum_fusion.4), channel_id=1, source_target_pairs={{0,1},{1,0},{2,3},{3,2},{4,5},{5,4},{6,7},{7,6},{8,9},{9,8},{10,11... | collective-permute-start | bytes 6152 | tf_op jit(solution)/shard_map/ppermute | solution.py:24

commit v2 on v1

--- a/solution.py
+++ b/solution.py
@@ -1,7 +1,10 @@
 import jax
 import jax.numpy as jnp
 from jax import lax
+from jax.experimental import pallas as pl
+from jax.experimental.pallas import tpu as pltpu
 from jax.sharding import PartitionSpec as P
+
 
 SEQ = 4096
 
@@ -94,7 +97,7 @@
     return high, low
 
 
-def per_device(
+def spread_device(
     latents, cotangent, routes, router_w, mod_shift, mod_scale, mod_gate, gate_w, up_w, down_w
 ):
     tok_rows, width = latents.shape
@@ -208,6 +211,313 @@
     )
 
 
+FEATURE_TILE = 512
+
+
+def after(value, *deps):
+    return lax.optimization_barrier((value,) + deps)[0]
+
+
+def dp_gather(value):
+    size = lax.axis_size("dp")
+    index = lax.axis_index("dp")
+    value = value[None]
+    step = 1
+    while step < size:
+        other = lax.ppermute(value, "dp", [(i, i ^ step) for i in range(size)])
+        low = (index & step) == 0
+        value = jnp.concatenate([jnp.where(low, value, other), jnp.where(low, other, value)])
+        step *= 2
+    return value
+
+
+def lin(rows, weight):
+    return jnp.dot(rows, weight, preferred_element_type=F32)
+
+
+def lin_t(rows, weight):
+    return lax.dot_general(rows, weight, (((1,), (1,)), ((), ())), preferred_element_type=F32)
+
+
+def lin_rows(left, right):
+    return lax.dot_general(left, right, (((0,), (0,)), ((), ())), preferred_element_type=F32)
+
+
+def expert_body(
+    core, own_x, oth_x, down_hbm, slot_w, coefs, router_own, router_oth, gate_hbm, up_hbm,
+    part_own, part_oth, gate_wt, up_wt, hidden_wt, high, low,
+    x_s, back_s, gate_s, up_s, own_s, oth_s, wt_s, sems, out_sems,
+):
+    width = own_x.shape[1]
+    halves = [pl.ds(place * width, width) for place in range(2)]
+    picked = [
+        pl.ds(pl.multiple_of(((core[0] + place) % 2) * width, width), width)
+        for place in range(2)
+    ]
+
+    def load(source, target, index, place):
+        copy = pltpu.make_async_copy(source, target, sems.at[index, place])
+        copy.start()
+        return copy
+
+    x_copies = [load(own_x, x_s.at[0], 0, 0)]
+    gate_copies = [load(gate_hbm.at[picked[0]], gate_s.at[halves[0]], 1, 0)]
+    x_copies.append(load(oth_x, x_s.at[1], 0, 1))
+    gate_copies.append(load(gate_hbm.at[picked[1]], gate_s.at[halves[1]], 1, 1))
+    up_copies = [load(up_hbm.at[picked[p]], up_s.at[halves[p]], 2, p) for p in range(2)]
+    back_copy = load(down_hbm, back_s, 3, 0)
+
+    def save(source, target, index):
+        copy = pltpu.make_async_copy(source, target, out_sems.at[index])
+        copy.start()
+        return copy
+
+    x_copies[0].wait()
+    gate_copies[0].wait()
+    gate_lin = lin(x_s[0], gate_s[:width])
+    x_copies[1].wait()
+    gate_copies[1].wait()
+    gate_lin = gate_lin + lin(x_s[1], gate_s[width:])
+    for copy in up_copies:
+        copy.wait()
+    up_lin = lin(x_s[0], up_s[:width]) + lin(x_s[1], up_s[width:])
+    back_copy.wait()
+    down_back = back_s[...]
+    gate_sig = jax.nn.sigmoid(gate_lin)
+    gate_act = gate_lin * gate_sig
+    hidden = gate_act * up_lin
+    scored = jnp.sum(hidden * down_back, axis=1, keepdims=True) * coefs[...]
+    scored_b = scored.astype(BF16)
+    high[...] = scored_b
+    low[...] = (scored - scored_b.astype(F32)).astype(BF16)
+    scale = slot_w[...]
+    wt_s[0] = (scale * down_back * up_lin * gate_sig * (1.0 + gate_lin * (1.0 - gate_sig))).astype(BF16)
+    wt_s[1] = (scale * down_back * gate_act).astype(BF16)
+    wt_s[2] = (scale * hidden).astype(BF16)
+    saves = [save(wt_s.at[k], ref, k) for k, ref in enumerate((gate_wt, up_wt, hidden_wt))]
+    oth_s[...] = (
+        lin_t(wt_s[0], gate_s[width:]) + lin_t(wt_s[1], up_s[width:]) + lin(scored_b, router_oth[...])
+    ).astype(BF16)
+    saves.append(save(oth_s, part_oth, 3))
+    own_s[...] = (
+        lin_t(wt_s[0], gate_s[:width]) + lin_t(wt_s[1], up_s[:width]) + lin(scored_b, router_own[...])
+    ).astype(BF16)
+    saves.append(save(own_s, part_own, 4))
+    for copy in saves:
+        copy.wait()
+
+
+def expert_rows(core, own_x, oth_x, down_back, slot_w, coefs, router_own, router_oth, gate_w, up_w):
+    rows, width = own_x.shape
+    hidden = gate_w.shape[1]
+    raw = pl.BlockSpec(memory_space=pl.ANY)
+    whole = pl.BlockSpec(memory_space=pltpu.VMEM)
+    wide = jax.ShapeDtypeStruct((rows, width), BF16)
+    deep = jax.ShapeDtypeStruct((rows, hidden), BF16)
+    narrow = jax.ShapeDtypeStruct(coefs.shape, BF16)
+    return pl.pallas_call(
+        expert_body,
+        name="expert_rows",
+        in_specs=[pl.BlockSpec(memory_space=pltpu.SMEM)] + [raw] * 3 + [whole] * 4 + [raw] * 2,
+        out_specs=[raw] * 5 + [whole] * 2,
+        scratch_shapes=[
+            pltpu.VMEM((2, rows, width), BF16),
+            pltpu.VMEM((rows, hidden), F32),
+            pltpu.VMEM((2 * width, hidden), BF16),
+            pltpu.VMEM((2 * width, hidden), BF16),
+            pltpu.VMEM((rows, width), BF16),
+            pltpu.VMEM((rows, width), BF16),
+            pltpu.VMEM((3, rows, hidden), BF16),
+            pltpu.SemaphoreType.DMA((4, 2)),
+            pltpu.SemaphoreType.DMA((5,)),
+        ],
+        out_shape=[wide, wide, deep, deep, deep, narrow, narrow],
+        cost_estimate=pl.CostEstimate(
+            flops=16 * rows * width * hidden,
+            bytes_accessed=8 * width * hidden + 8 * rows * width + 10 * rows * hidden,
+            transcendentals=rows * hidden,
+        ),
+    )(core, own_x, oth_x, down_back, slot_w, coefs, router_own, router_oth, gate_w, up_w)
+
+
+def router_body(own_x, oth_x, high, low, own, oth):
+    for rows, out in ((own_x, own), (oth_x, oth)):
+        out[...] = lin_rows(high[...], rows[...]) + lin_rows(low[...], rows[...])
+
+
+def router_grads(own_x, oth_x, high, low):
+    rows, width = own_x.shape
+    experts = high.shape[1]
+    out = jax.ShapeDtypeStruct((experts, width), F32)
+    return pl.pallas_call(
+        router_body,
+        name="router_grads",
+        out_shape=[out, out],
+        cost_estimate=pl.CostEstimate(
+            flops=8 * rows * width * experts,
+            bytes_accessed=4 * rows * width,
+            transcendentals=0,
+        ),
+    )(own_x, oth_x, high, low)
+
+
+def weight_body(core, own_x, oth_x, own_z, oth_z, gate_wt, up_wt, hidden_wt, *grads):
+    grad_gate, grad_up, grad_down = grads
+
+    def write(x_rows, z_rows):
+        grad_gate[...] = lin_rows(x_rows[...], gate_wt[...]).astype(BF16)
+        grad_up[...] = lin_rows(x_rows[...], up_wt[...]).astype(BF16)
+        grad_down[...] = lin_rows(hidden_wt[...], z_rows[...]).astype(BF16)
+
+    @pl.when(pl.program_id(0) == 0)
+    def _():
+        write(own_x, own_z)
+
+    @pl.when(pl.program_id(0) == 1)
+    def _():
+        write(oth_x, oth_z)
+
+
+def weight_grads(core, own_x, oth_x, own_z, oth_z, gate_wt, up_wt, hidden_wt):
+    rows, width = own_x.shape
+    hidden = gate_wt.shape[1]
+    tile = FEATURE_TILE if width % FEATURE_TILE == 0 else width
+    steps = width // tile
+    own = pl.BlockSpec((rows, tile), lambda h, i, core: (0, jnp.where(h == 0, i, steps - 1)))
+    oth = pl.BlockSpec((rows, tile), lambda h, i, core: (0, jnp.where(h == 0, 0, i)))
+    full = pl.BlockSpec((rows, hidden), lambda h, i, core: (0, 0))
+    by_rows = pl.BlockSpec((tile, hidden), lambda h, i, core: (((core[0] + h) % 2) * steps + i, 0))
+    by_columns = pl.BlockSpec((hidden, tile), lambda h, i, core: (0, ((core[0] + h) % 2) * steps + i))
+    tall = jax.ShapeDtypeStruct((2 * width, hidden), BF16)
+    return pl.pallas_call(
+        weight_body,
+        name="weight_grads",
+        grid_spec=pltpu.PrefetchScalarGridSpec(
+            num_scalar_prefetch=1,
+            grid=(2, steps),
+            in_specs=[own, oth, own, oth] + [full] * 3,
+            out_specs=[by_rows, by_rows, by_columns],
+        ),
+        out_shape=[tall, tall, jax.ShapeDtypeStruct((hidden, 2 * width), BF16)],
+        cost_estimate=pl.CostEstimate(
+            flops=12 * rows * width * hidden,
+            bytes_accessed=12 * width * hidden + 8 * rows * width + 6 * rows * hidden,
+            transcendentals=0,
+        ),
+    )(core, own_x, oth_x, own_z, oth_z, gate_wt, up_wt, hidden_wt)
+
+
+def per_device(
+    latents, cotangent, routes, router_w, mod_shift, mod_scale, mod_gate, gate_w, up_w, down_w
+):
+    size = lax.axis_size("dp")
+    if lax.axis_size("expert") != 2 or size & (size - 1) or gate_w.shape[0] != 1:
+        return spread_device(
+            latents, cotangent, routes, router_w, mod_shift, mod_scale, mod_gate,
+            gate_w, up_w, down_w,
+        )
+    tok_rows, width = latents.shape
+    experts = router_w.shape[1]
+    entire_width = 2 * width
+    capacity = 3 * tok_rows // experts
+    slot_count = experts * capacity
+    dp_index = lax.axis_index("dp")
+    sample_index = dp_index * tok_rows // SEQ
+    core = lax.axis_index("expert").astype(jnp.int32).reshape(1)
+    gate_w, up_w, down_w = gate_w[0], up_w[0], down_w[0]
+
+    expert_ids = lax.broadcasted_iota(jnp.int32, (experts, tok_rows), 0)
+    named = [routes[:, k][None, :] == expert_ids for k in range(2)]
+    named_b = (named[0] | named[1]).astype(BF16)
+    rows_i = lax.broadcasted_iota(jnp.int32, (tok_rows, tok_rows), 0)
+    cols_i = lax.broadcasted_iota(jnp.int32, (tok_rows, tok_rows), 1)
+    places = lin(named_b, (rows_i < cols_i).astype(BF16)) + (expert_ids * capacity).astype(F32)
+    targets = [jnp.sum(jnp.where(n, places, 0.0), axis=0) for n in named]
+    slot_ids = lax.broadcasted_iota(jnp.int32, (slot_count, tok_rows), 0).astype(F32)
+    fill = ((targets[0][None, :] == slot_ids) | (targets[1][None, :] == slot_ids)).astype(BF16)
+
+    def to_slots(rows_b):
+        return lin(fill, rows_b).astype(BF16).reshape(experts, capacity, width)
+
+    cot = cotangent.astype(F32)
+    scaled_dy = (selected_row(mod_gate, sample_index) * cot).astype(BF16)
+    send_z = to_slots(scaled_dy)
+    latents = after(latents, send_z)
+    own_z = all_to_all(send_z).reshape(slot_count, width)
+
+    x = latents.astype(F32)
+    sums = jnp.stack([jnp.sum(x, axis=1), jnp.sum(x * x, axis=1)])
+    mean, msq = core_sum(sums) / entire_width
+    inv_std = lax.rsqrt(msq - mean * mean + norm_eps)[:, None]
+    xhat = (x - mean[:, None]) * inv_std
+    amp = 1.0 + selected_row(mod_scale, sample_index)
+    normed = xhat * amp + selected_row(mod_shift, sample_index)
+    send_x = to_slots(normed.astype(BF16))
+    own_x = all_to_all(send_x).reshape(slot_count, width)
+
+    logits = core_sum(lax.dot_general(
+        router_w, normed, (((0,), (1,)), ((), ())), precision=HIGHEST
+    ))
+    chances = jax.nn.sigmoid(logits)
+    picked = jnp.stack([jnp.sum(jnp.where(n, chances, 0.0), axis=0) for n in named])
+    pick_sum = jnp.sum(picked, axis=0, keepdims=True)
+    weights = picked / pick_sum
+    slopes = weights[::-1] * picked * (1.0 - picked) / pick_sum
+    other_ids = routes.T[::-1].astype(F32)
+    slot_row = lax.broadcasted_iota(jnp.int32, (tok_rows, slot_count), 1).astype(F32)
+    hits = [t[:, None] == slot_row for t in targets]
+
+    def of_slots(pair):
+        return jnp.sum(
+            jnp.where(hits[0], pair[0][:, None], 0.0) + jnp.where(hits[1], pair[1][:, None], 0.0),
+            axis=0,
+        ).reshape(experts, capacity)
+
+    kinds = (weights, slopes, slopes[::-1], other_ids)
+    sent = jnp.concatenate([of_slots(pair) for pair in kinds], axis=1)
+    arrived = lax.dynamic_index_in_dim(dp_gather(sent), dp_index, 1, keepdims=False)
+    slot_w, slope, slope_other, other = [
+        arrived[:, k * capacity:(k + 1) * capacity].reshape(slot_count, 1) for k in range(4)
+    ]
+    ids = lax.broadcasted_iota(jnp.int32, (slot_count, experts), 1).astype(F32)
+    coefs = jnp.where(ids == dp_index.astype(F32), slope, 0.0) - jnp.where(
+        ids == other, slope_other, 0.0
+    )
+    router_own = router_w.T.astype(BF16)
+    router_oth = pair_swap(router_own)
+    join = (hits[0] | hits[1]).astype(BF16)
+
+    oth_z = pair_swap(own_z)
+    down_own = lax.dynamic_slice_in_dim(down_w, core[0] * width, width, 1)
+    down_oth = lax.dynamic_slice_in_dim(down_w, (1 - core[0]) * width, width, 1)
+    down_back = lin_t(own_z, down_own) + lin_t(oth_z, down_oth)
+    own_x, down_back, slot_w, coefs, join = lax.optimization_barrier(
+        (own_x, down_back, slot_w, coefs, join)
+    )
+
+    oth_x = pair_swap(own_x)
+    part_own, part_oth, gate_wt, up_wt, hidden_wt, high, low = expert_rows(
+        core, own_x, oth_x, down_back, slot_w, coefs, router_own, router_oth, gate_w, up_w
+    )
+    send_back = (part_own.astype(F32) + pair_swap(part_oth).astype(F32)).astype(BF16)
+    back = all_to_all(send_back.reshape(experts, capacity, width)).reshape(slot_count, width)
+
+    router_own, router_oth = router_grads(own_x, oth_x, high, low)
+    grad_gate, grad_up, grad_down = weight_grads(
+        core, own_x, oth_x, own_z, oth_z, gate_wt, up_wt, hidden_wt
+    )
+    grad_router = dp_sum(router_own + pair_swap(router_oth)).T
+
+    dxhat = lin(join, back) * amp
+    m_one, m_two = core_sum(
+        jnp.stack([jnp.sum(dxhat, axis=1), jnp.sum(dxhat * xhat, axis=1)])
+    ) / entire_width
+    latent_gradient = inv_std * (dxhat - m_one[:, None] - xhat * m_two[:, None]) + cot
+    return (
+        latent_gradient.astype(BF16), grad_gate[None], grad_up[None], grad_down[None], grad_router
+    )
+
+
 def solution(mesh):
     placed = (
         P("dp", "expert"),

time: 198 us -> 179 us (0.904)
  the two profiles are of different devices: /device:TPU:13 before, /device:TPU:0 now
where the time goes in v2:
time: 179 us; the launch traced here: 177 us
  waiting for transfers between devices  77.8 us (43%)
  starting transfers between devices  43.9 us (25%)
  Pallas kernels  27.5 us (15%)
  matrix products  14.2 us (8%)
  other arithmetic  9.56 us (5%)
  local copies, waits for them, and re-layouts  3.22 us (2%)
    all_to_all x3, waiting for transfers between devices, all_to_all(): return lax.all_to_all(value, 'dp', split_axis=0, concat_axis=0, tiled=True)  30.5 us
    ppermute x4, waiting for transfers between devices, dp_gather(): other = lax.ppermute(value, 'dp', [(i, i ^ step) for i in range(size)])  30.4 us
    all_to_all x3, starting transfers between devices, all_to_all(): return lax.all_to_all(value, 'dp', split_axis=0, concat_axis=0, tiled=True)  21.2 us
    pallas_call x1, Pallas kernels, expert_rows(): pl.pallas_call(expert_body, name='expert_rows', in_specs=[pl.BlockSpec(me...  14 us
    ppermute x4, starting transfers between devices, dp_sum(): lax.ppermute(value, 'dp', [(i, i ^ step) for i in range(size)])  10.9 us
    ppermute x4, starting transfers between devices, dp_gather(): other = lax.ppermute(value, 'dp', [(i, i ^ step) for i in range(size)])  10.6 us
    pallas_call x1, Pallas kernels, weight_grads(): pl.pallas_call(weight_body, name='weight_grads', grid_spec=pltpu.Prefetch...  10 us
    ppermute x4, waiting for transfers between devices, dp_sum(): lax.ppermute(value, 'dp', [(i, i ^ step) for i in range(size)])  8.68 us
  transfers between devices with their start and end apart: 19, of which 13 were waited for; matrix products, arithmetic and copies ran while one was open for 10% of the time, Pallas kernels for 8%

profile of v2, /device:TPU:0, one launch (start us, length us, event | category | flops | bytes accessed | tf_op | source)
XLA Modules:
  0.0 177.2 jit_solution(13920871538979676536)
XLA Ops:
  0.6 0.0 copy-start
  0.7 0.8 mul.109
  1.5 0.8 fusion.59
  2.3 0.1 select_reduce_fusion.3
  2.4 2.8 %convolution_convert_fusion.1 = bf16[768,1024]{1,0:T(8,128)(2,1)} fusion(bf16[256,1024]{1,0:T(8,128)(2,1)} %param.11, f32[1024]{0:T(1024)S(1)} %bitcast.77, f32[256]{0:T(256)S(1)} %get-tuple-element.48, f32[256]{0:T(256)S(1)} %get-tuple-element.47, f32[768]{0:T(1024)S(1)} %iota_convert_fusion), kind=kOutput, calls=%fused_computation.2 | convolution fusion | flops 404815872 | bytes 2106368 | tf_op jit(solution)/shard_map/dot_general | solution.py:235
  5.3 8.5 %all-to-all-start.1 = ((bf16[16,48,1024]{2,1,0:T(8,128)(2,1)}), bf16[16,48,1024]{2,1,0:T(8,128)(2,1)}, u32[]{:S(2)}, u32[]{:S(2)}) async-start(bf16[16,48,1024]{2,1,0:T(8,128)(2,1)} %bitcast.55), calls=%async_computation.1 | async-start | bytes 3145728 | tf_op jit(solution)/shard_map/all_to_all | solution.py:73
  13.8 0.2 convert_reduce_fusion
  14.1 0.1 collective-permute-start
  14.2 0.1 rev.8
  14.3 1.0 collective-permute-done
  15.3 1.1 convolution_bitcast_fusion
  16.4 0.2 collective-permute-start.2
  16.6 1.9 %convolution_convert_fusion = bf16[768,1024]{1,0:T(8,128)(2,1)} fusion(bf16[256,1024]{1,0:T(8,128)(2,1)S(1)} %copy-done.1, f32[1024]{0:T(1024)S(1)} %bitcast.76, f32[1024]{0:T(1024)S(1)} %bitcast.73, f32[256]{0:T(256)S(1)} %bitcast.62, f32[256]{0:T(256)S(1)} %add_rsqrt_fusion, f32[256]{0:T(256)S(1)} %get-tuple-element.48, f32[256]{0:T(256)S(1)} %get-tuple-element.47, ...), kind=kOutput, calls=%fused_computation.1 | convolution fusion | flops 405602304 | bytes 2112512 | tf_op jit(solution)/shard_map/dot_general | solution.py:235
  18.6 0.1 rev.7
  18.8 0.6 fusion.21
  19.3 0.1 reshape.99
  19.4 0.1 reshape.98
  19.5 0.1 reshape.97
  19.5 0.1 reshape.96
  19.6 28.3 %all-to-all-done.1 = bf16[16,48,1024]{2,1,0:T(8,128)(2,1)} async-done(((bf16[16,48,1024]{2,1,0:T(8,128)(2,1)}), bf16[16,48,1024]{2,1,0:T(8,128)(2,1)}, u32[]{:S(2)}, u32[]{:S(2)}) %all-to-all-start.1) | async-done | bytes 1572896 | tf_op jit(solution)/shard_map/all_to_all | solution.py:73
  48.0 7.8 %all-to-all-start = ((bf16[16,48,1024]{2,1,0:T(8,128)(2,1)}), bf16[16,48,1024]{2,1,0:T(8,128)(2,1)}, u32[]{:S(2)}, u32[]{:S(2)}) async-start(bf16[16,48,1024]{2,1,0:T(8,128)(2,1)} %bitcast.54), calls=%async_computation | async-start | bytes 3145728 | tf_op jit(solution)/shard_map/all_to_all | solution.py:73
  55.8 0.1 pad_maximum_fusion.3
  55.9 1.9 %collective-permute-start.3 = (f32[1,16,192]{2,0,1:T(1,128)S(1)}, f32[1,16,192]{2,0,1:T(1,128)S(1)}, u32[]{:S(2)}, u32[]{:S(2)}) collective-permute-start(f32[1,16,192]{2,0,1:T(1,128)S(1)} %broadcast_in_dim.123), channel_id=1, source_target_pairs={{0,2},{2,0},{4,6},{6,4},{8,10},{10,8},{12,14},{14,12},{16,18},{18,... | collective-permute-start | bytes 36872 | tf_op jit(solution)/shard_map/ppermute | solution.py:227
  57.8 3.9 %collective-permute-done.3 = f32[1,16,192]{2,0,1:T(1,128)S(1)} collective-permute-done((f32[1,16,192]{2,0,1:T(1,128)S(1)}, f32[1,16,192]{2,0,1:T(1,128)S(1)}, u32[]{:S(2)}, u32[]{:S(2)}) %collective-permute-start.3) | collective-permute-done | bytes 12320 | tf_op jit(solution)/shard_map/ppermute | solution.py:227
  61.8 2.0 %collective-permute-start.4 = (f32[2,16,192]{2,0,1:T(2,128)S(1)}, f32[2,16,192]{2,0,1:T(2,128)S(1)}, u32[]{:S(2)}, u32[]{:S(2)}) collective-permute-start(f32[2,16,192]{2,0,1:T(2,128)S(1)} %pad_maximum_fusion.2), channel_id=1, source_target_pairs={{0,4},{2,6},{4,0},{6,2},{8,12},{10,14},{12,8},{14,10},{16,20},{18,... | collective-permute-start | bytes 73736 | tf_op jit(solution)/shard_map/ppermute | solution.py:227
  63.8 0.2 fusion.26
  64.0 2.0 %collective-permute-done.4 = f32[2,16,192]{2,0,1:T(2,128)S(1)} collective-permute-done((f32[2,16,192]{2,0,1:T(2,128)S(1)}, f32[2,16,192]{2,0,1:T(2,128)S(1)}, u32[]{:S(2)}, u32[]{:S(2)}) %collective-permute-start.4) | collective-permute-done | bytes 24608 | tf_op jit(solution)/shard_map/ppermute | solution.py:227
  66.0 1.5 collective-permute-start.5
  67.5 14.1 %collective-permute-done.5 = f32[4,16,192]{2,0,1:T(4,128)S(1)} collective-permute-done((f32[4,16,192]{2,0,1:T(4,128)S(1)}, f32[4,16,192]{2,0,1:T(4,128)S(1)}, u32[]{:S(2)}, u32[]{:S(2)}) %collective-permute-start.5) | collective-permute-done | bytes 49184 | tf_op jit(solution)/shard_map/ppermute | solution.py:227
  81.7 5.2 %collective-permute-start.6 = (f32[8,16,192]{2,0,1:T(8,128)S(1)}, f32[8,16,192]{2,0,1:T(8,128)S(1)}, u32[]{:S(2)}, u32[]{:S(2)}) collective-permute-start(f32[8,16,192]{2,0,1:T(8,128)S(1)} %pad_maximum_fusion), channel_id=1, source_target_pairs={{0,16},{2,18},{4,20},{6,22},{8,24},{10,26},{12,28},{14,30},{16,0},... | collective-permute-start | bytes 294920 | tf_op jit(solution)/shard_map/ppermute | solution.py:227
  86.9 10.5 %collective-permute-done.6 = f32[8,16,192]{2,0,1:T(8,128)S(1)} collective-permute-done((f32[8,16,192]{2,0,1:T(8,128)S(1)}, f32[8,16,192]{2,0,1:T(8,128)S(1)}, u32[]{:S(2)}, u32[]{:S(2)}) %collective-permute-start.6) | collective-permute-done | bytes 98336 | tf_op jit(solution)/shard_map/ppermute | solution.py:227
  97.5 0.1 fusion.53
  97.6 0.1 reshape.100
  97.6 0.1 broadcast_in_dim.127
  97.7 0.1 broadcast_in_dim.124
  97.8 0.1 eq.101
  97.9 1.1 select_subtract_fusion.coefs
  99.0 2.4 %fusion.14 = f32[768,512]{1,0:T(8,128)S(1)} fusion(bf16[768,1024]{1,0:T(8,128)(2,1)} %bitcast.12.own_z, bf16[1,512,2048]{2,1,0:T(8,128)(2,1)S(1)} %copy-done, s32[]{:T(128)S(6)} %select_n.111), kind=kOutput, calls=%fused_computation.34 | convolution fusion | flops 805306368 | bytes 4194308 | tf_op jit(solution)/shard_map/dot_general | solution.py:239
  101.4 3.6 %convolution_add_fusion.down_hbm = f32[768,512]{1,0:T(8,128)} fusion(f32[768,512]{1,0:T(8,128)S(1)} %fusion.14, bf16[768,1024]{1,0:T(8,128)(2,1)} %collective-permute-done.1.oth_z, bf16[1,512,2048]{2,1,0:T(8,128)(2,1)S(1)} %copy-done, s32[]{:T(128)S(6)} %select_n.112), kind=kOutput, calls=%fused_computation.15 | convolution fusion | flops 805699584 | bytes 5767172 | tf_op jit(solution)/shard_map/dot_general | solution.py:239
  105.1 0.6 collective-permute-start.8
  105.6 0.9 copy.16.slot_w
  106.6 2.2 %collective-permute-done.8.router_oth = bf16[16,1024]{1,0:T(8,128)(2,1)S(1)} collective-permute-done((bf16[16,1024]{1,0:T(8,128)(2,1)S(1)}, bf16[16,1024]{1,0:T(8,128)(2,1)S(1)}, u32[]{:S(2)}, u32[]{:S(2)}) %collective-permute-start.8) | collective-permute-done | bytes 32800 | tf_op jit(solution)/shard_map/ppermute | solution.py:27
  108.8 0.6 copy-done.8
  109.4 14.0 %expert_rows.1 = (bf16[768,1024]{1,0:T(8,128)(2,1)}, bf16[768,1024]{1,0:T(8,128)(2,1)}, bf16[768,512]{1,0:T(8,128)(2,1)}, bf16[768,512]{1,0:T(8,128)(2,1)}, bf16...) custom-call(s32[1]{0:T(128)} %bitcast.26.core, bf16[768,1024]{1,0:T(8,128)(2,1)} %bitcast.11.own_x, ...), custom_call_target="tpu_custom_call" | custom-call | flops 6442450944 | bytes 14417920 | tf_op jit(solution)/shard_map/expert_rows/pallas_call | solution.py:318
  123.4 0.2 collective-permute-start.9
  123.6 3.5 %collective-permute-done.9 = bf16[768,1024]{1,0:T(8,128)(2,1)S(1)} collective-permute-done((bf16[768,1024]{1,0:T(8,128)(2,1)}, bf16[768,1024]{1,0:T(8,128)(2,1)S(1)}, u32[]{:S(2)}, u32[]{:S(2)}) %collective-permute-start.9) | collective-permute-done | bytes 1572896 | tf_op jit(solution)/shard_map/ppermute | solution.py:27
  127.1 3.3 %add_convert_fusion = bf16[768,1024]{1,0:T(8,128)(2,1)} fusion(bf16[768,1024]{1,0:T(8,128)(2,1)S(1)} %collective-permute-done.9, bf16[768,1024]{1,0:T(8,128)(2,1)} %get-tuple-element.29), kind=kLoop, calls=%fused_computation | loop fusion | flops 3145728 | bytes 4718592 | tf_op jit(solution)/shard_map/convert_element_type | solution.py:502
  130.4 4.9 %all-to-all-start.2 = ((bf16[16,48,1024]{2,1,0:T(8,128)(2,1)}), bf16[16,48,1024]{2,1,0:T(8,128)(2,1)}, u32[]{:S(2)}, u32[]{:S(2)}) async-start(bf16[16,48,1024]{2,1,0:T(8,128)(2,1)} %bitcast.53), calls=%async_computation.2 | async-start | bytes 3145728 | tf_op jit(solution)/shard_map/all_to_all | solution.py:73
  135.3 3.5 %router_grads.1 = (f32[16,1024]{1,0:T(8,128)}, f32[16,1024]{1,0:T(8,128)}) custom-call(bf16[768,1024]{1,0:T(8,128)(2,1)} %bitcast.11.own_x, bf16[768,1024]{1,0:T(8,128)(2,1)} %collective-permute-done.7.oth_x, bf16[768,16]{1,0:T(8,128)(2,1)} %get-tuple-element.37.high, bf16[768,16]{1,0:T(8,128)(2,1)} %get-tuple-element.38.low), custom_call_target="tpu_custom_call" | custom-call | flops 100663296 | bytes 3145728 | tf_op jit(solution)/shard_map/router_grads/pallas_call | solution.py:352
  138.8 1.5 collective-permute-done.11
  140.3 0.9 add.117
  141.2 1.9 %collective-permute-start.12 = (f32[16,1024]{1,0:T(8,128)S(1)}, f32[16,1024]{1,0:T(8,128)S(1)}, u32[]{:S(2)}, u32[]{:S(2)}) collective-permute-start(f32[16,1024]{1,0:T(8,128)S(1)} %add.117), channel_id=1, source_target_pairs={{0,2},{2,0},{4,6},{6,4},{8,10},{10,8},{12,14},{14,12},{16,18},{18,... | collective-permute-start | bytes 196616 | tf_op jit(solution)/shard_map/ppermute | solution.py:67
  143.1 2.4 %collective-permute-done.12 = f32[16,1024]{1,0:T(8,128)S(1)} collective-permute-done((f32[16,1024]{1,0:T(8,128)S(1)}, f32[16,1024]{1,0:T(8,128)S(1)}, u32[]{:S(2)}, u32[]{:S(2)}) %collective-permute-start.12) | collective-permute-done | bytes 65568 | tf_op jit(solution)/shard_map/ppermute | solution.py:67
  145.5 2.5 %collective-permute-start.13 = (f32[16,1024]{1,0:T(8,128)S(1)}, f32[16,1024]{1,0:T(8,128)S(1)}, u32[]{:S(2)}, u32[]{:S(2)}) collective-permute-start(f32[16,1024]{1,0:T(8,128)S(1)} %add.118), channel_id=1, source_target_pairs={{0,4},{2,6},{4,0},{6,2},{8,12},{10,14},{12,8},{14,10},{16,20},{18,... | collective-permute-start | bytes 196616 | tf_op jit(solution)/shard_map/ppermute | solution.py:67
  148.0 2.5 %collective-permute-done.13 = f32[16,1024]{1,0:T(8,128)S(1)} collective-permute-done((f32[16,1024]{1,0:T(8,128)S(1)}, f32[16,1024]{1,0:T(8,128)S(1)}, u32[]{:S(2)}, u32[]{:S(2)}) %collective-permute-start.13) | collective-permute-done | bytes 65568 | tf_op jit(solution)/shard_map/ppermute | solution.py:67
  150.5 3.8 %collective-permute-start.14 = (f32[16,1024]{1,0:T(8,128)S(1)}, f32[16,1024]{1,0:T(8,128)S(1)}, u32[]{:S(2)}, u32[]{:S(2)}) collective-permute-start(f32[16,1024]{1,0:T(8,128)S(1)} %add.119), channel_id=1, source_target_pairs={{0,8},{2,10},{4,12},{6,14},{8,0},{10,2},{12,4},{14,6},{16,24},{18,... | collective-permute-start | bytes 196616 | tf_op jit(solution)/shard_map/ppermute | solution.py:67
  154.4 10.0 %weight_grads.1 = (bf16[2048,512]{1,0:T(8,128)(2,1)}, bf16[2048,512]{1,0:T(8,128)(2,1)}, bf16[512,2048]{1,0:T(8,128)(2,1)}) custom-call(s32[1]{0:T(128)} %bitcast.26.core, bf16[768,1024]{1,0:T(8,128)(2,1)} %bitcast.11.own_x, bf16[768,1024]{1,0:T(8,128)(2,1)} %collective-permute-done.7.oth_x, bf16[768,1024]{1,0:T(8,128)(2,1)} %bitcast.12.own_z, ...), custom_call_target="tpu_custom_call" | custom-call | flops 4831838208 | bytes 14942208 | tf_op jit(solution)/shard_map/weight_grads/pallas_call | solution.py:392
  164.4 2.7 %collective-permute-start.15 = (f32[16,1024]{1,0:T(8,128)S(1)}, f32[16,1024]{1,0:T(8,128)S(1)}, u32[]{:S(2)}, u32[]{:S(2)}) collective-permute-start(f32[16,1024]{1,0:T(8,128)S(1)} %add.120), channel_id=1, source_target_pairs={{0,16},{2,18},{4,20},{6,22},{8,24},{10,26},{12,28},{14,30},{16,0},... | collective-permute-start | bytes 196616 | tf_op jit(solution)/shard_map/ppermute | solution.py:67
  167.1 2.2 %all-to-all-done.2 = bf16[16,48,1024]{2,1,0:T(8,128)(2,1)} async-done(((bf16[16,48,1024]{2,1,0:T(8,128)(2,1)}), bf16[16,48,1024]{2,1,0:T(8,128)(2,1)}, u32[]{:S(2)}, u32[]{:S(2)}) %all-to-all-start.2) | async-done | bytes 1572896 | tf_op jit(solution)/shard_map/all_to_all | solution.py:73
  169.3 2.2 %fusion.52 = (f32[256]{0:T(256)S(1)}, f32[256]{0:T(256)S(1)}, f32[256,1024]{1,0:T(8,128)S(1)}) fusion(f32[256]{0:T(256)S(1)} %add_rsqrt_fusion, f32[256]{0:T(256)S(1)} %bitcast.63, bf16[256,1024]{1,0:T(8,128)(2,1)S(1)} %copy-done.1, f32[1024]{0:T(1024)S(1)} %bitcast.74, bf16[256,768]{1,0:T(8,128)(2,1)S(1)} %fusion.26, bf16[768,1024]{1,0:T(8,128)(2,1)} %bitcast.31), kind=kOutput, calls=%fused_computation.108 | convolution fusion | flops 404487680 | bytes 3547136 | tf_op jit(solution)/shard_map/dot_general | solution.py:235
  171.5 0.1 collective-permute-start.10
  171.6 3.8 %collective-permute-done.15 = f32[16,1024]{1,0:T(8,128)S(1)} collective-permute-done((f32[16,1024]{1,0:T(8,128)S(1)}, f32[16,1024]{1,0:T(8,128)S(1)}, u32[]{:S(2)}, u32[]{:S(2)}) %collective-permute-start.15) | collective-permute-done | bytes 65568 | tf_op jit(solution)/shard_map/ppermute | solution.py:67
  175.3 0.6 add_bitcast_fusion
  176.0 1.2 fusion.1
  (59 shorter events, 0.6 us)
Async XLA Ops:
  0.6 98.4 %copy-start = (bf16[1,512,2048]{2,1,0:T(8,128)(2,1)S(1)}, bf16[1,512,2048]{2,1,0:T(8,128)(2,1)}, u32[]{:S(2)}) copy-start(bf16[1,512,2048]{2,1,0:T(8,128)(2,1)} %param.19) | copy-start | bytes 6291460
  5.2 8.6 %copy-start.1 = (bf16[256,1024]{1,0:T(8,128)(2,1)S(1)}, bf16[256,1024]{1,0:T(8,128)(2,1)}, u32[]{:S(2)}) copy-start(bf16[256,1024]{1,0:T(8,128)(2,1)} %param.10) | copy-start | bytes 1572868
  5.2 8.9 %copy-start.5 = (s32[256,2]{0,1:T(2,128)S(1)}, s32[256,2]{0,1:T(2,128)}, u32[]{:S(2)}) copy-start(s32[256,2]{0,1:T(2,128)} %param.12) | copy-start | bytes 6148
  5.2 9.0 %copy-start.6 = (bf16[1,1024]{1,0:T(2,128)(2,1)S(1)}, bf16[1,1024]{1,0:T(2,128)(2,1)}, u32[]{:S(2)}) copy-start(bf16[1,1024]{1,0:T(2,128)(2,1)} %param.15) | copy-start | bytes 6148
  5.2 9.1 %copy-start.7 = (bf16[1,1024]{1,0:T(2,128)(2,1)S(1)}, bf16[1,1024]{1,0:T(2,128)(2,1)}, u32[]{:S(2)}) copy-start(bf16[1,1024]{1,0:T(2,128)(2,1)} %param.14) | copy-start | bytes 6148
  5.2 10.1 %copy-start.3 = (f32[1024,16]{0,1:T(8,128)S(1)}, f32[1024,16]{0,1:T(8,128)}, u32[]{:S(2)}) copy-start(f32[1024,16]{0,1:T(8,128)} %param.13) | copy-start | bytes 196612
  5.3 42.7 %all-to-all-start.1 = ((bf16[16,48,1024]{2,1,0:T(8,128)(2,1)}), bf16[16,48,1024]{2,1,0:T(8,128)(2,1)}, u32[]{:S(2)}, u32[]{:S(2)}) async-start(bf16[16,48,1024]{2,1,0:T(8,128)(2,1)} %bitcast.55), calls=%async_computation.1 | async-start | bytes 3145728 | tf_op jit(solution)/shard_map/all_to_all | solution.py:73
  14.1 1.2 collective-permute-start
  16.4 2.1 %collective-permute-start.2 = (f32[16,256]{1,0:T(8,128)S(1)}, f32[16,256]{1,0:T(8,128)S(1)}, u32[]{:S(2)}, u32[]{:S(2)}) collective-permute-start(f32[16,256]{1,0:T(8,128)S(1)} %convolution_bitcast_fusion), channel_id=1, source_target_pairs={{0,1},{1,0},{2,3},{3,2},{4,5},{5,4},{6,7},{7,6},{8,9},{9,8},{10,11... | collective-permute-start | bytes 49160 | tf_op jit(solution)/shard_map/ppermute | solution.py:27
  48.0 57.1 %all-to-all-start = ((bf16[16,48,1024]{2,1,0:T(8,128)(2,1)}), bf16[16,48,1024]{2,1,0:T(8,128)(2,1)}, u32[]{:S(2)}, u32[]{:S(2)}) async-start(bf16[16,48,1024]{2,1,0:T(8,128)(2,1)} %bitcast.54), calls=%async_computation | async-start | bytes 3145728 | tf_op jit(solution)/shard_map/all_to_all | solution.py:73
  55.9 5.8 %collective-permute-start.3 = (f32[1,16,192]{2,0,1:T(1,128)S(1)}, f32[1,16,192]{2,0,1:T(1,128)S(1)}, u32[]{:S(2)}, u32[]{:S(2)}) collective-permute-start(f32[1,16,192]{2,0,1:T(1,128)S(1)} %broadcast_in_dim.123), channel_id=1, source_target_pairs={{0,2},{2,0},{4,6},{6,4},{8,10},{10,8},{12,14},{14,12},{16,18},{18,... | collective-permute-start | bytes 36872 | tf_op jit(solution)/shard_map/ppermute | solution.py:227
  61.8 4.2 %collective-permute-start.4 = (f32[2,16,192]{2,0,1:T(2,128)S(1)}, f32[2,16,192]{2,0,1:T(2,128)S(1)}, u32[]{:S(2)}, u32[]{:S(2)}) collective-permute-start(f32[2,16,192]{2,0,1:T(2,128)S(1)} %pad_maximum_fusion.2), channel_id=1, source_target_pairs={{0,4},{2,6},{4,0},{6,2},{8,12},{10,14},{12,8},{14,10},{16,20},{18,... | collective-permute-start | bytes 73736 | tf_op jit(solution)/shard_map/ppermute | solution.py:227
  66.0 15.6 %collective-permute-start.5 = (f32[4,16,192]{2,0,1:T(4,128)S(1)}, f32[4,16,192]{2,0,1:T(4,128)S(1)}, u32[]{:S(2)}, u32[]{:S(2)}) collective-permute-start(f32[4,16,192]{2,0,1:T(4,128)S(1)} %pad_maximum_fusion.1), channel_id=1, source_target_pairs={{0,8},{2,10},{4,12},{6,14},{8,0},{10,2},{12,4},{14,6},{16,24},{18,... | collective-permute-start | bytes 147464 | tf_op jit(solution)/shard_map/ppermute | solution.py:227
  67.5 33.9 %collective-permute-start.1 = (bf16[768,1024]{1,0:T(8,128)(2,1)}, bf16[768,1024]{1,0:T(8,128)(2,1)}, u32[]{:S(2)}, u32[]{:S(2)}) collective-permute-start(bf16[768,1024]{1,0:T(8,128)(2,1)} %bitcast.12.own_z), channel_id=1, source_target_pairs={{0,1},{1,0},{2,3},{3,2},{4,5},{5,4},{6,7},{7,6},{8,9},{9,8},{10,11... | collective-permute-start | bytes 4718600 | tf_op jit(solution)/shard_map/ppermute | solution.py:27
  81.7 15.7 %collective-permute-start.6 = (f32[8,16,192]{2,0,1:T(8,128)S(1)}, f32[8,16,192]{2,0,1:T(8,128)S(1)}, u32[]{:S(2)}, u32[]{:S(2)}) collective-permute-start(f32[8,16,192]{2,0,1:T(8,128)S(1)} %pad_maximum_fusion), channel_id=1, source_target_pairs={{0,16},{2,18},{4,20},{6,22},{8,24},{10,26},{12,28},{14,30},{16,0},... | collective-permute-start | bytes 294920 | tf_op jit(solution)/shard_map/ppermute | solution.py:227
  105.0 3.8 %collective-permute-start.7 = (bf16[768,1024]{1,0:T(8,128)(2,1)}, bf16[768,1024]{1,0:T(8,128)(2,1)}, u32[]{:S(2)}, u32[]{:S(2)}) collective-permute-start(bf16[768,1024]{1,0:T(8,128)(2,1)} %bitcast.11.own_x), channel_id=1, source_target_pairs={{0,1},{1,0},{2,3},{3,2},{4,5},{5,4},{6,7},{7,6},{8,9},{9,8},{10,11... | collective-permute-start | bytes 4718600 | tf_op jit(solution)/shard_map/ppermute | solution.py:27
  105.0 3.7 %copy-start.4 = (bf16[16,1024]{1,0:T(8,128)(2,1)}, bf16[16,1024]{1,0:T(8,128)(2,1)S(1)}, u32[]{:S(2)}) copy-start(bf16[16,1024]{1,0:T(8,128)(2,1)S(1)} %convert_bitcast_fusion.router_own) | copy-start | bytes 98308
  105.1 3.7 %collective-permute-start.8 = (bf16[16,1024]{1,0:T(8,128)(2,1)S(1)}, bf16[16,1024]{1,0:T(8,128)(2,1)S(1)}, u32[]{:S(2)}, u32[]{:S(2)}) collective-permute-start(bf16[16,1024]{1,0:T(8,128)(2,1)S(1)} %convert_bitcast_fusion.router_own), channel_id=1, source_target_pairs={{0,1},{1,0},{2,3},{3,2},{4,5},{5,4},{6,7},{7,6},{8,9},{9,8},{10,11... | collective-permute-start | bytes 98312 | tf_op jit(solution)/shard_map/ppermute | solution.py:27
  108.8 0.6 copy-start.8
  123.4 3.7 %collective-permute-start.9 = (bf16[768,1024]{1,0:T(8,128)(2,1)}, bf16[768,1024]{1,0:T(8,128)(2,1)S(1)}, u32[]{:S(2)}, u32[]{:S(2)}) collective-permute-start(bf16[768,1024]{1,0:T(8,128)(2,1)} %get-tuple-element.30), channel_id=1, source_target_pairs={{0,1},{1,0},{2,3},{3,2},{4,5},{5,4},{6,7},{7,6},{8,9},{9,8},{10,11... | collective-permute-start | bytes 4718600 | tf_op jit(solution)/shard_map/ppermute | solution.py:27
  130.4 38.8 %all-to-all-start.2 = ((bf16[16,48,1024]{2,1,0:T(8,128)(2,1)}), bf16[16,48,1024]{2,1,0:T(8,128)(2,1)}, u32[]{:S(2)}, u32[]{:S(2)}) async-start(bf16[16,48,1024]{2,1,0:T(8,128)(2,1)} %bitcast.53), calls=%async_computation.2 | async-start | bytes 3145728 | tf_op jit(solution)/shard_map/all_to_all | solution.py:73
  138.8 1.5 collective-permute-start.11
  141.2 4.3 %collective-permute-start.12 = (f32[16,1024]{1,0:T(8,128)S(1)}, f32[16,1024]{1,0:T(8,128)S(1)}, u32[]{:S(2)}, u32[]{:S(2)}) collective-permute-start(f32[16,1024]{1,0:T(8,128)S(1)} %add.117), channel_id=1, source_target_pairs={{0,2},{2,0},{4,6},{6,4},{8,10},{10,8},{12,14},{14,12},{16,18},{18,... | collective-permute-start | bytes 196616 | tf_op jit(solution)/shard_map/ppermute | solution.py:67
  145.5 5.0 %collective-permute-start.13 = (f32[16,1024]{1,0:T(8,128)S(1)}, f32[16,1024]{1,0:T(8,128)S(1)}, u32[]{:S(2)}, u32[]{:S(2)}) collective-permute-start(f32[16,1024]{1,0:T(8,128)S(1)} %add.118), channel_id=1, source_target_pairs={{0,4},{2,6},{4,0},{6,2},{8,12},{10,14},{12,8},{14,10},{16,20},{18,... | collective-permute-start | bytes 196616 | tf_op jit(solution)/shard_map/ppermute | solution.py:67
  150.5 13.9 %collective-permute-start.14 = (f32[16,1024]{1,0:T(8,128)S(1)}, f32[16,1024]{1,0:T(8,128)S(1)}, u32[]{:S(2)}, u32[]{:S(2)}) collective-permute-start(f32[16,1024]{1,0:T(8,128)S(1)} %add.119), channel_id=1, source_target_pairs={{0,8},{2,10},{4,12},{6,14},{8,0},{10,2},{12,4},{14,6},{16,24},{18,... | collective-permute-start | bytes 196616 | tf_op jit(solution)/shard_map/ppermute | solution.py:67
  164.4 10.9 %collective-permute-start.15 = (f32[16,1024]{1,0:T(8,128)S(1)}, f32[16,1024]{1,0:T(8,128)S(1)}, u32[]{:S(2)}, u32[]{:S(2)}) collective-permute-start(f32[16,1024]{1,0:T(8,128)S(1)} %add.120), channel_id=1, source_target_pairs={{0,16},{2,18},{4,20},{6,22},{8,24},{10,26},{12,28},{14,30},{16,0},... | collective-permute-start | bytes 196616 | tf_op jit(solution)/shard_map/ppermute | solution.py:67
  169.3 6.7 %copy-start.2 = (bf16[256,1024]{1,0:T(8,128)(2,1)S(1)}, bf16[256,1024]{1,0:T(8,128)(2,1)}, u32[]{:S(2)}) copy-start(bf16[256,1024]{1,0:T(8,128)(2,1)} %param.11) | copy-start | bytes 1572868
  171.5 4.5 %collective-permute-start.10 = (f32[2,256]{1,0:T(2,128)S(1)}, f32[2,256]{1,0:T(2,128)S(1)}, u32[]{:S(2)}, u32[]{:S(2)}) collective-permute-start(f32[2,256]{1,0:T(2,128)S(1)} %pad_maximum_fusion.6), channel_id=1, source_target_pairs={{0,1},{1,0},{2,3},{3,2},{4,5},{5,4},{6,7},{7,6},{8,9},{9,8},{10,11... | collective-permute-start | bytes 6152 | tf_op jit(solution)/shard_map/ppermute | solution.py:27
